TPU v7x, 128 devices: a whole 4x4x4 slice. The times are simulated.
128 devices in a mesh: frame: 2 (over x_hi), height: 8 (over z, core), width: 8 (over y, x_lo).
Axes of the slice: x: 4 (x_hi: 2, x_lo: 2; x = x_hi * 2 + x_lo), y: 4, z: 4, core: 2. Of those that a mesh axis runs over, the one named last changes fastest.
Arguments:
- activations: bfloat16 [8, 128, 256, 256], P('frame', 'height', 'width'), may hold values from -6 to 6
- out_grad: bfloat16 [8, 128, 256, 256], P('frame', 'height', 'width'), may hold values from -40 to 40
- kernel: bfloat16 [6912, 256], P(('frame', 'height', 'width')), may hold values from -5 to 5
- damping: float32 [], replicated, may hold values from 0.02 to 0.2
Outputs:
- input_grad: bfloat16 [8, 128, 256, 256], P('frame', 'height', 'width')
- new_kernel: bfloat16 [6912, 256], replicated
All inputs are finite; a program needn't handle non-finite values.
Results may differ from a plain program's by a relative error of at most 0.001.
Values may be sent and summed in bfloat16 or wider, within the bound.
A program may use at most 192 MiB of HBM per device.

v0:
```python
import jax
import jax.numpy as jnp
from jax import lax
from jax.sharding import Mesh
from jax.sharding import PartitionSpec as P

ITERS = 12
FRAME_HEIGHT_WIDTH = ("frame", "height_0", "height_1", "width_0", "width_1")
HEIGHT = ("height_0", "height_1")
WIDTH = ("width_0", "width_1")


def cut_rows(length, count):
    turn = length // count
    if turn >= 8:
        turn -= turn % 8
    return [turn * k for k in range(1, count)]


def gather_in_order(value, axes, turns):
    blocks = value
    for k in turns:
        blocks = lax.all_gather(blocks, axes[k])
    done = turns[::-1]
    back = [done.index(k) for k in range(len(axes))]
    blocks = blocks.transpose(*back, *range(len(axes), blocks.ndim))
    return blocks.reshape(-1, *value.shape)


def joined_along(blocks, dim):
    shape = list(blocks.shape[1:])
    shape[dim] *= blocks.shape[0]
    return jnp.moveaxis(blocks, 0, dim).reshape(shape)


def spread_gather(value, axes, dim):
    widest = max(range(max(1, value.ndim - 1)), key=lambda d: value.shape[d])
    count, gathered = (len(axes), [])
    for initial, slab in enumerate(
        jnp.split(value, cut_rows(value.shape[widest], count), axis=widest)
    ):
        if slab.size:
            turns = [(initial - k) % count for k in range(count)]
            gathered.append(gather_in_order(slab, axes, turns))
    return joined_along(jnp.concatenate(gathered, axis=widest + 1), dim)


def with_halo(cells, sides, width):
    for axis, dim in sides:
        count = lax.axis_size(axis)
        ends = count - 1
        head = lax.slice_in_dim(cells, 0, width, axis=dim)
        tail = lax.slice_in_dim(cells, cells.shape[dim] - width, cells.shape[dim], axis=dim)
        cells = jnp.concatenate(
            [
                lax.ppermute(tail, axis, [(i, (i + 1) % count) for i in range(ends)]),
                cells,
                lax.ppermute(head, axis, [((i + 1) % count, i) for i in range(ends)]),
            ],
            axis=dim,
        )
    return cells


def newton_root(gram, damping):
    order = gram.shape[0]
    identity = jnp.eye(order, dtype=jnp.float32)
    factor = gram + damping * (jnp.trace(gram) / order) * identity
    start_scale = 2.5 / jnp.sqrt(jnp.sum(factor * factor))
    inverse_root = jnp.sqrt(jnp.sqrt(start_scale)) * identity
    matrix = start_scale * factor
    for step in range(ITERS):
        middle = (5.0 * identity - matrix) / 4.0
        inverse_root = jnp.dot(inverse_root, middle, precision=lax.Precision.HIGHEST)
        square = jnp.dot(middle, middle, precision=lax.Precision.HIGHEST)
        matrix = jnp.dot(
            square,
            jnp.dot(square, matrix, precision=lax.Precision.HIGHEST),
            precision=lax.Precision.HIGHEST,
        )
    return inverse_root


def gram_of(rows):
    return lax.dot_general(rows, rows, (((0,), (0,)), ((), ())), precision=lax.Precision.HIGHEST)


def on_device(activations, out_grad, kernel, damping):
    frames, height, width, chans = activations.shape
    count = frames * height * width
    full_kernel = spread_gather(kernel, FRAME_HEIGHT_WIDTH, 0)
    padded_in = with_halo(activations, (("frame", 0), (HEIGHT, 1), (WIDTH, 2)), 1)
    padded_grad = with_halo(out_grad, (("frame", 0), (HEIGHT, 1), (WIDTH, 2)), 1)
    flat_grad = out_grad.reshape(count, chans)
    pieces = []
    total = jnp.zeros((count, chans), jnp.float32)
    for tap_f in range(3):
        for tap_h in range(3):
            for tap_w in range(3):
                tap = 9 * tap_f + 3 * tap_h + tap_w
                shifted = padded_in[
                    tap_f : tap_f + frames, tap_h : tap_h + height, tap_w : tap_w + width
                ].reshape(count, chans)
                pieces.append(
                    lax.dot_general(
                        shifted,
                        flat_grad,
                        (((0,), (0,)), ((), ())),
                        preferred_element_type=jnp.float32,
                    )
                )
                back = padded_grad[
                    2 - tap_f : 2 - tap_f + frames,
                    2 - tap_h : 2 - tap_h + height,
                    2 - tap_w : 2 - tap_w + width,
                ].reshape(count, chans)
                total = total + jnp.dot(
                    back,
                    full_kernel[tap * chans : (tap + 1) * chans],
                    preferred_element_type=jnp.float32,
                )
    krows = full_kernel.shape[0]
    input_grad = (
        (total / jnp.sqrt(jnp.float32(krows)))
        .astype(jnp.bfloat16)
        .reshape(frames, height, width, chans)
    )
    partial_value = jnp.concatenate(pieces, 0)
    entries = krows * chans
    kernel_grad = lax.psum(partial_value, FRAME_HEIGHT_WIDTH)
    inverse_root = newton_root(gram_of(kernel_grad), damping)
    direction = jnp.dot(kernel_grad, inverse_root, precision=lax.Precision.HIGHEST)
    size = jnp.sqrt(jnp.sum(direction * direction) / entries + 1e-06)
    new_kernel = (full_kernel.astype(jnp.float32) - 0.5 * direction / size).astype(jnp.bfloat16)
    return (input_grad, new_kernel)


def solution(mesh):
    torus = Mesh(
        mesh.devices.reshape(mesh.shape["frame"], 4, 2, 4, 2),
        ("frame", "height_0", "height_1", "width_0", "width_1"),
    )
    placed = (
        P("frame", HEIGHT, WIDTH, None),
        P("frame", HEIGHT, WIDTH, None),
        P(FRAME_HEIGHT_WIDTH, None),
        P(),
    )
    return jax.shard_map(
        on_device,
        mesh=torus,
        in_specs=placed,
        out_specs=(P("frame", HEIGHT, WIDTH, None), P()),
        check_vma=False,
    )
```

profile of v0, /device:TPU:1, one launch (start us, length us, event | category | flops | bytes accessed | tf_op | source)
XLA Modules:
  0.0 516.6 jit_solution(16949379575316959948)
XLA Ops:
  10.0 6.2 %collective-permute-start.6 = (bf16[1,16,32,256]{3,2,1,0:T(8,128)(2,1)}, bf16[1,16,32,256]{3,2,1,0:T(8,128)(2,1)}, u32[]{:S(2)}, u32[]{:S(2)}) collective-permute-start(bf16[1,16,32,256]{3,2,1,0:T(8,128)(2,1)} %get-tuple-element.42), channel_id=1, source_target_pairs={{0,64},{1,65},{2,66},{3,67},{4,68},{5,69},{6,70},{7,71},{8,72},{9,... | collective-permute-start | bytes 786440 | tf_op jit(solution)/shard_map/ppermute | solution.py:56
  21.7 10.3 %all-gather.21 = bf16[8,22,256]{2,1,0:T(8,128)(2,1)S(1)} all-gather(bf16[2,22,256]{2,1,0:T(8,128)(2,1)S(1)} %all-gather.25), channel_id=23, replica_groups=mesh['frame'=2,'height_0'=4,'height_1'=2,'width_0'=4,'width_1'=2] {'widt..., dimensions={0}, use_global_device_ids=true | all-gather | bytes 112640 | tf_op jit(solution)/shard_map/all_gather | solution.py:23
  32.1 5.5 %all-gather.22 = bf16[8,2,22,256]{3,1,2,0:T(2,128)(2,1)S(1)} all-gather(bf16[4,2,22,256]{3,1,2,0:T(2,128)(2,1)S(1)} %copy.39), channel_id=24, replica_groups=mesh['frame'=2,'height_0'=4,'height_1'=2,'width_0'=4,'width_1'=2] {'heig..., dimensions={0}, use_global_device_ids=true | all-gather | bytes 270336 | tf_op jit(solution)/shard_map/all_gather | solution.py:23
  37.7 13.4 %all-gather.23 = bf16[8,4,2,22,256]{4,1,3,2,0:T(4,128)(2,1)} all-gather(bf16[2,4,2,22,256]{4,1,3,2,0:T(4,128)(2,1)S(1)} %copy.40), channel_id=25, replica_groups=mesh['frame'=2,'height_0'=4,'height_1'=2,'width_0'=4,'width_1'=2] {'heig..., dimensions={0}, use_global_device_ids=true | all-gather | bytes 901120 | tf_op jit(solution)/shard_map/all_gather | solution.py:23
  52.0 8.1 %collective-permute-start = (bf16[1,16,32,256]{3,2,1,0:T(8,128)(2,1)}, bf16[1,16,32,256]{3,2,1,0:T(8,128)(2,1)S(1)}, u32[]{:S(2)}, u32[]{:S(2)}) collective-permute-start(bf16[1,16,32,256]{3,2,1,0:T(8,128)(2,1)} %get-tuple-element.47), channel_id=1, source_target_pairs={{0,64},{1,65},{2,66},{3,67},{4,68},{5,69},{6,70},{7,71},{8,72},{9,... | collective-permute-start | bytes 786440 | tf_op jit(solution)/shard_map/ppermute | solution.py:56
  61.4 7.6 %all-gather = bf16[16,256]{1,0:T(8,128)(2,1)S(1)} all-gather(bf16[8,256]{1,0:T(8,128)(2,1)S(1)} %get-tuple-element.51), channel_id=2, replica_groups=mesh['frame'=2,'height_0'=4,'height_1'=2,'width_0'=4,'width_1'=2] {'frame'}, dimensions={0}, use_global_device_ids=true | all-gather | bytes 12288 | tf_op jit(solution)/shard_map/all_gather | solution.py:23
  69.1 3.9 all-gather.1
  72.9 10.2 %all-gather.2 = bf16[8,2,8,256]{3,2,1,0:T(8,128)(2,1)S(1)} all-gather(bf16[2,2,8,256]{3,2,1,0:T(8,128)(2,1)S(1)} %bitcast.405), channel_id=4, replica_groups=mesh['frame'=2,'height_0'=4,'height_1'=2,'width_0'=4,'width_1'=2] {'widt..., dimensions={0}, use_global_device_ids=true | all-gather | bytes 81920 | tf_op jit(solution)/shard_map/all_gather | solution.py:23
  83.1 8.7 %all-gather.3 = bf16[8,2,2,8,256]{4,3,2,1,0:T(8,128)(2,1)S(1)} all-gather(bf16[4,2,2,8,256]{4,3,2,1,0:T(8,128)(2,1)S(1)} %bitcast.397), channel_id=5, replica_groups=mesh['frame'=2,'height_0'=4,'height_1'=2,'width_0'=4,'width_1'=2] {'heig..., dimensions={0}, use_global_device_ids=true | all-gather | bytes 196608 | tf_op jit(solution)/shard_map/all_gather | solution.py:23
  91.8 12.9 %all-gather.4 = bf16[8,4,2,2,8,256]{5,4,3,2,1,0:T(8,128)(2,1)S(1)} all-gather(bf16[2,4,2,2,8,256]{5,4,3,2,1,0:T(8,128)(2,1)S(1)} %bitcast.394), channel_id=6, replica_groups=mesh['frame'=2,'height_0'=4,'height_1'=2,'width_0'=4,'width_1'=2] {'heig..., dimensions={0}, use_global_device_ids=true | all-gather | bytes 655360 | tf_op jit(solution)/shard_map/all_gather | solution.py:23
  106.3 9.1 %all-gather.5 = bf16[32,256]{1,0:T(8,128)(2,1)S(1)} all-gather(bf16[8,256]{1,0:T(8,128)(2,1)S(1)} %get-tuple-element.50), channel_id=7, replica_groups=mesh['frame'=2,'height_0'=4,'height_1'=2,'width_0'=4,'width_1'=2] {'heig..., dimensions={0}, use_global_device_ids=true | all-gather | bytes 20480 | tf_op jit(solution)/shard_map/all_gather | solution.py:23
  115.4 4.7 all-gather.6
  123.6 9.4 %all-gather.8 = bf16[8,2,4,8,256]{4,3,2,1,0:T(8,128)(2,1)S(1)} all-gather(bf16[2,2,4,8,256]{4,3,2,1,0:T(8,128)(2,1)S(1)} %bitcast.398), channel_id=10, replica_groups=mesh['frame'=2,'height_0'=4,'height_1'=2,'width_0'=4,'width_1'=2] {'widt..., dimensions={0}, use_global_device_ids=true | all-gather | bytes 327680 | tf_op jit(solution)/shard_map/all_gather | solution.py:23
  132.9 12.0 %all-gather.9 = bf16[8,2,2,4,8,256]{5,4,3,2,1,0:T(8,128)(2,1)S(1)} all-gather(bf16[4,2,2,4,8,256]{5,4,3,2,1,0:T(8,128)(2,1)S(1)} %bitcast.390), channel_id=11, replica_groups=mesh['frame'=2,'height_0'=4,'height_1'=2,'width_0'=4,'width_1'=2] {'heig..., dimensions={0}, use_global_device_ids=true | all-gather | bytes 786432 | tf_op jit(solution)/shard_map/all_gather | solution.py:23
  147.5 9.4 %all-gather.11 = bf16[8,8,256]{2,1,0:T(8,128)(2,1)S(1)} all-gather(bf16[2,8,256]{2,1,0:T(8,128)(2,1)S(1)} %bitcast.407), channel_id=13, replica_groups=mesh['frame'=2,'height_0'=4,'height_1'=2,'width_0'=4,'width_1'=2] {'heig..., dimensions={0}, use_global_device_ids=true | all-gather | bytes 40960 | tf_op jit(solution)/shard_map/all_gather | solution.py:23
  156.9 4.9 all-gather.12
  165.6 9.9 %all-gather.14 = bf16[8,2,4,2,8,256]{5,4,3,2,1,0:T(8,128)(2,1)S(1)} all-gather(bf16[2,2,4,2,8,256]{5,4,3,2,1,0:T(8,128)(2,1)S(1)} %bitcast.395), channel_id=16, replica_groups=mesh['frame'=2,'height_0'=4,'height_1'=2,'width_0'=4,'width_1'=2] {'widt..., dimensions={0}, use_global_device_ids=true | all-gather | bytes 655360 | tf_op jit(solution)/shard_map/all_gather | solution.py:23
  176.2 9.4 %all-gather.15 = bf16[32,256]{1,0:T(8,128)(2,1)S(1)} all-gather(bf16[8,256]{1,0:T(8,128)(2,1)S(1)} %get-tuple-element.48), channel_id=17, replica_groups=mesh['frame'=2,'height_0'=4,'height_1'=2,'width_0'=4,'width_1'=2] {'widt..., dimensions={0}, use_global_device_ids=true | all-gather | bytes 20480 | tf_op jit(solution)/shard_map/all_gather | solution.py:23
  185.6 12.2 %all-gather.16 = bf16[8,8,256]{2,1,0:T(8,128)(2,1)S(1)} all-gather(bf16[4,8,256]{2,1,0:T(8,128)(2,1)S(1)} %bitcast.404), channel_id=18, replica_groups=mesh['frame'=2,'height_0'=4,'height_1'=2,'width_0'=4,'width_1'=2] {'heig..., dimensions={0}, use_global_device_ids=true | all-gather | bytes 49152 | tf_op jit(solution)/shard_map/all_gather | solution.py:23
  197.8 9.6 %all-gather.17 = bf16[8,4,8,256]{3,2,1,0:T(8,128)(2,1)S(1)} all-gather(bf16[2,4,8,256]{3,2,1,0:T(8,128)(2,1)S(1)} %bitcast.402), channel_id=19, replica_groups=mesh['frame'=2,'height_0'=4,'height_1'=2,'width_0'=4,'width_1'=2] {'heig..., dimensions={0}, use_global_device_ids=true | all-gather | bytes 163840 | tf_op jit(solution)/shard_map/all_gather | solution.py:23
  207.4 6.0 %all-gather.18 = bf16[8,2,4,8,256]{4,3,2,1,0:T(8,128)(2,1)S(1)} all-gather(bf16[4,2,4,8,256]{4,3,2,1,0:T(8,128)(2,1)S(1)} %bitcast.393), channel_id=20, replica_groups=mesh['frame'=2,'height_0'=4,'height_1'=2,'width_0'=4,'width_1'=2] {'frame'}, dimensions={0}, use_global_device_ids=true | all-gather | bytes 393216 | tf_op jit(solution)/shard_map/all_gather | solution.py:23
  213.4 5.9 %all-gather.19 = bf16[4,4,2,4,8,256]{5,4,3,2,1,0:T(8,128)(2,1)S(1)} all-gather(bf16[2,4,2,4,8,256]{5,4,3,2,1,0:T(8,128)(2,1)S(1)} %bitcast.391), channel_id=21, replica_groups=mesh['frame'=2,'height_0'=4,'height_1'=2,'width_0'=4,'width_1'=2] {'widt..., dimensions={0}, use_global_device_ids=true | all-gather | bytes 786432 | tf_op jit(solution)/shard_map/all_gather | solution.py:23
  224.6 10.0 %collective-permute-start.8 = (bf16[6,1,32,256]{3,2,1,0:T(8,128)(2,1)S(1)}, bf16[6,1,32,256]{3,2,1,0:T(8,128)(2,1)S(1)}, u32[]{:S(2)}, u32[]{:S(2)}) collective-permute-start(bf16[6,1,32,256]{3,2,1,0:T(8,128)(2,1)S(1)} %get-tuple-element.34), channel_id=1, source_target_pairs={{0,8},{8,16},{16,24},{24,32},{32,40},{40,48},{48,56},{1,9},{9,17},... | collective-permute-start | bytes 294920 | tf_op jit(solution)/shard_map/ppermute | solution.py:56
  251.3 4.5 collective-permute-start.5
  295.8 8.1 %fusion.310 = (bf16[4,16,32,256]{3,2,1,0:T(8,128)(2,1)}, bf16[4,16,32,256]{3,2,1,0:T(8,128)(2,1)}, bf16[4,16,32,256]{3,2,1,0:T(8,128)(2,1)}, bf16[4,16,32,256]{3...) fusion(bf16[6,18,33,256]{3,2,1,0:T(8,128)(2,1)S(1)} %get-tuple-, ...), kind=kLoop, calls=%fused_computation.384 | loop fusion | bytes 37748736 | tf_op jit(solution)/shard_map/slice | solution.py:112
  304.0 4.0 copy.41
  312.7 6.0 %copy.43 = bf16[128,54,256]{2,1,0:T(8,128)(2,1)} copy(bf16[128,54,256]{2,0,1:T(8,128)(2,1)} %constant_dynamic-update-slice_fusion.3) | data formatting | bytes 7077888 | tf_op jit(solution)/shard_map/concatenate | solution.py:45
  318.6 6.5 %reshape.140 = bf16[6912,256]{1,0:T(8,128)(2,1)} reshape(bf16[128,54,256]{2,1,0:T(8,128)(2,1)} %copy.43) | data formatting | bytes 7077888 | tf_op jit(solution)/shard_map/reshape | solution.py:33
  357.1 96.6 %all-reduce.2.cloned.1.call-done = f32[6912,256]{1,0:T(8,128)} async-done(((f32[6912,256]{1,0:T(8,128)}), f32[6912,256]{1,0:T(8,128)}) %all-reduce.2.cloned.1.call-update) | async-done | bytes 7077904 | tf_op jit(solution)/shard_map/psum | solution.py:130
  453.7 16.8 %select_reduce_fusion = (f32[]{:T(128)}, f32[256,256]{1,0:T(8,128)S(1)}) fusion(f32[6912,256]{1,0:T(8,128)} %all-reduce.2.cloned.1.call-done), kind=kOutput, calls=%fused_computation.165 | convolution fusion | flops 5436014592 | bytes 7340036 | tf_op jit(solution)/shard_map/dot_general | solution.py:85
  491.0 10.4 %multiply_reduce_fusion = (f32[]{:T(128)}, f32[6912,256]{1,0:T(8,128)}) fusion(f32[6912,256]{1,0:T(8,128)} %all-reduce.2.cloned.1.call-done, f32[256,256]{1,0:T(8,128)S(1)} %fusion.337), kind=kOutput, calls=%fused_computation.1 | convolution fusion | flops 5439356928 | bytes 14417924 | tf_op jit(solution)/shard_map/dot_general | solution.py:132
  502.2 6.8 %subtract_convert_fusion = bf16[6912,256]{1,0:T(8,128)(2,1)} fusion(f32[6912,256]{1,0:T(8,128)} %get-tuple-element.55, bf16[6912,256]{1,0:T(8,128)(2,1)} %reshape.140, f32[]{:T(128)S(6)} %sqrt.15), kind=kLoop, calls=%fused_computation | loop fusion | flops 8847360 | bytes 14155780 | tf_op jit(solution)/shard_map/convert_element_type | solution.py:134
  (221 shorter events, 138.0 us)
Async XLA Ops:
  8.0 53.4 %copy-start.29 = (bf16[54,256]{1,0:T(8,128)(2,1)S(1)}, bf16[54,256]{1,0:T(8,128)(2,1)}, u32[]{:S(2)}) copy-start(bf16[54,256]{1,0:T(8,128)(2,1)} %param.6) | copy-start | bytes 82948
  8.0 43.2 %copy-start = (bf16[4,16,32,256]{3,2,1,0:T(8,128)(2,1)S(1)}, bf16[4,16,32,256]{3,2,1,0:T(8,128)(2,1)}, u32[]{:S(2)}) copy-start(bf16[4,16,32,256]{3,2,1,0:T(8,128)(2,1)} %param.5) | copy-start | bytes 3145732
  8.0 296.0 %all-gather.28.cloned.1.call-start = ((), (), s32[]{:S(2)}) async-start(), calls=%async_computation.1 | async-start | bytes 2162688 | tf_op jit(solution)/shard_map/all_gather | solution.py:23
  10.0 212.5 %collective-permute-start.6 = (bf16[1,16,32,256]{3,2,1,0:T(8,128)(2,1)}, bf16[1,16,32,256]{3,2,1,0:T(8,128)(2,1)}, u32[]{:S(2)}, u32[]{:S(2)}) collective-permute-start(bf16[1,16,32,256]{3,2,1,0:T(8,128)(2,1)} %get-tuple-element.42), channel_id=1, source_target_pairs={{0,64},{1,65},{2,66},{3,67},{4,68},{5,69},{6,70},{7,71},{8,72},{9,... | collective-permute-start | bytes 786440 | tf_op jit(solution)/shard_map/ppermute | solution.py:56
  16.2 207.4 %collective-permute-start.7 = (bf16[1,16,32,256]{3,2,1,0:T(8,128)(2,1)}, bf16[1,16,32,256]{3,2,1,0:T(8,128)(2,1)}, u32[]{:S(2)}, u32[]{:S(2)}) collective-permute-start(bf16[1,16,32,256]{3,2,1,0:T(8,128)(2,1)} %get-tuple-element.41), channel_id=1, source_target_pairs={{64,0},{65,1},{66,2},{67,3},{68,4},{69,5},{70,6},{71,7},{72,8},{73... | collective-permute-start | bytes 786440 | tf_op jit(solution)/shard_map/ppermute | solution.py:58
  51.1 402.6 %all-reduce.2.cloned.1.call-start = ((), (), s32[]{:S(2)}) async-start(), calls=%async_computation | async-start | bytes 14155776 | tf_op jit(solution)/shard_map/psum | solution.py:130
  52.0 184.5 %collective-permute-start = (bf16[1,16,32,256]{3,2,1,0:T(8,128)(2,1)}, bf16[1,16,32,256]{3,2,1,0:T(8,128)(2,1)S(1)}, u32[]{:S(2)}, u32[]{:S(2)}) collective-permute-start(bf16[1,16,32,256]{3,2,1,0:T(8,128)(2,1)} %get-tuple-element.47), channel_id=1, source_target_pairs={{0,64},{1,65},{2,66},{3,67},{4,68},{5,69},{6,70},{7,71},{8,72},{9,... | collective-permute-start | bytes 786440 | tf_op jit(solution)/shard_map/ppermute | solution.py:56
  60.1 176.4 %collective-permute-start.1 = (bf16[1,16,32,256]{3,2,1,0:T(8,128)(2,1)}, bf16[1,16,32,256]{3,2,1,0:T(8,128)(2,1)}, u32[]{:S(2)}, u32[]{:S(2)}) collective-permute-start(bf16[1,16,32,256]{3,2,1,0:T(8,128)(2,1)} %get-tuple-element.46), channel_id=1, source_target_pairs={{64,0},{65,1},{66,2},{67,3},{68,4},{69,5},{70,6},{71,7},{72,8},{73... | collective-permute-start | bytes 786440 | tf_op jit(solution)/shard_map/ppermute | solution.py:58
  219.2 4.2 copy-start.2
  224.6 21.2 %collective-permute-start.8 = (bf16[6,1,32,256]{3,2,1,0:T(8,128)(2,1)S(1)}, bf16[6,1,32,256]{3,2,1,0:T(8,128)(2,1)S(1)}, u32[]{:S(2)}, u32[]{:S(2)}) collective-permute-start(bf16[6,1,32,256]{3,2,1,0:T(8,128)(2,1)S(1)} %get-tuple-element.34), channel_id=1, source_target_pairs={{0,8},{8,16},{16,24},{24,32},{32,40},{40,48},{48,56},{1,9},{9,17},... | collective-permute-start | bytes 294920 | tf_op jit(solution)/shard_map/ppermute | solution.py:56
  234.6 11.3 %collective-permute-start.9 = (bf16[6,1,32,256]{3,2,1,0:T(8,128)(2,1)S(1)}, bf16[6,1,32,256]{3,2,1,0:T(8,128)(2,1)S(1)}, u32[]{:S(2)}, u32[]{:S(2)}) collective-permute-start(bf16[6,1,32,256]{3,2,1,0:T(8,128)(2,1)S(1)} %get-tuple-element.35), channel_id=1, source_target_pairs={{8,0},{16,8},{24,16},{32,24},{40,32},{48,40},{56,48},{9,1},{17,9},... | collective-permute-start | bytes 294920 | tf_op jit(solution)/shard_map/ppermute | solution.py:58
  240.2 8.7 %collective-permute-start.2 = (bf16[6,1,32,256]{3,2,1,0:T(8,128)(2,1)S(1)}, bf16[6,1,32,256]{3,2,1,0:T(8,128)(2,1)S(1)}, u32[]{:S(2)}, u32[]{:S(2)}) collective-permute-start(bf16[6,1,32,256]{3,2,1,0:T(8,128)(2,1)S(1)} %get-tuple-element.39), channel_id=1, source_target_pairs={{0,8},{8,16},{16,24},{24,32},{32,40},{40,48},{48,56},{1,9},{9,17},... | collective-permute-start | bytes 294920 | tf_op jit(solution)/shard_map/ppermute | solution.py:56
  243.9 5.9 %collective-permute-start.3 = (bf16[6,1,32,256]{3,2,1,0:T(8,128)(2,1)S(1)}, bf16[6,1,32,256]{3,2,1,0:T(8,128)(2,1)S(1)}, u32[]{:S(2)}, u32[]{:S(2)}) collective-permute-start(bf16[6,1,32,256]{3,2,1,0:T(8,128)(2,1)S(1)} %get-tuple-element.40), channel_id=1, source_target_pairs={{8,0},{16,8},{24,16},{32,24},{40,32},{48,40},{56,48},{9,1},{17,9},... | collective-permute-start | bytes 294920 | tf_op jit(solution)/shard_map/ppermute | solution.py:58
  246.0 12.6 %collective-permute-start.10 = (bf16[6,18,1,256]{3,2,1,0:T(2,128)(2,1)S(1)}, bf16[6,18,1,256]{3,2,1,0:T(2,128)(2,1)S(1)}, u32[]{:S(2)}, u32[]{:S(2)}) collective-permute-start(bf16[6,18,1,256]{3,2,1,0:T(2,128)(2,1)S(1)} %get-tuple-element.23), channel_id=1, source_target_pairs={{0,1},{1,2},{2,3},{3,4},{4,5},{5,6},{6,7},{8,9},{9,10},{10,11},{11... | collective-permute-start | bytes 165896 | tf_op jit(solution)/shard_map/ppermute | solution.py:56
  247.7 11.0 %collective-permute-start.11 = (bf16[6,18,1,256]{3,2,1,0:T(2,128)(2,1)S(1)}, bf16[6,18,1,256]{3,2,1,0:T(2,128)(2,1)S(1)}, u32[]{:S(2)}, u32[]{:S(2)}) collective-permute-start(bf16[6,18,1,256]{3,2,1,0:T(2,128)(2,1)S(1)} %get-tuple-element.22), channel_id=1, source_target_pairs={{1,0},{2,1},{3,2},{4,3},{5,4},{6,5},{7,6},{9,8},{10,9},{11,10},{12... | collective-permute-start | bytes 165896 | tf_op jit(solution)/shard_map/ppermute | solution.py:58
  250.0 44.1 %collective-permute-start.4 = (bf16[6,18,1,256]{3,2,1,0:T(2,128)(2,1)S(1)}, bf16[6,18,1,256]{3,2,1,0:T(2,128)(2,1)S(1)}, u32[]{:S(2)}, u32[]{:S(2)}) collective-permute-start(bf16[6,18,1,256]{3,2,1,0:T(2,128)(2,1)S(1)} %get-tuple-element.26), channel_id=1, source_target_pairs={{1,0},{2,1},{3,2},{4,3},{5,4},{6,5},{7,6},{9,8},{10,9},{11,10},{12... | collective-permute-start | bytes 165896 | tf_op jit(solution)/shard_map/ppermute | solution.py:58
  251.3 42.8 %collective-permute-start.5 = (bf16[6,18,1,256]{3,2,1,0:T(2,128)(2,1)S(1)}, bf16[6,18,1,256]{3,2,1,0:T(2,128)(2,1)S(1)}, u32[]{:S(2)}, u32[]{:S(2)}) collective-permute-start(bf16[6,18,1,256]{3,2,1,0:T(2,128)(2,1)S(1)} %get-tuple-element.27), channel_id=1, source_target_pairs={{0,1},{1,2},{2,3},{3,4},{4,5},{5,6},{6,7},{8,9},{9,10},{10,11},{11... | collective-permute-start | bytes 165896 | tf_op jit(solution)/shard_map/ppermute | solution.py:56
  262.4 2.4 copy-start.3
  318.6 6.5 %copy-start.6 = (bf16[4,16,32,256]{3,2,1,0:T(8,128)(2,1)S(1)}, bf16[4,16,32,256]{3,2,1,0:T(8,128)(2,1)}, u32[]{:S(2)}) copy-start(bf16[4,16,32,256]{3,2,1,0:T(8,128)(2,1)} %get-tuple-element.37) | copy-start | bytes 3145732
  325.1 1.5 copy-start.9
  325.1 3.0 copy-start.1
  326.7 1.6 copy-start.8
  328.1 1.3 copy-start.7
  328.6 1.4 copy-start.28
  331.2 1.3 copy-start.26
  332.5 1.3 copy-start.11
  338.7 1.3 copy-start.13
  342.9 1.2 copy-start.20
  344.6 1.2 copy-start.19
  347.0 1.2 copy-start.18
  350.7 1.2 copy-start.16
  352.0 1.2 copy-start.10
  (12 other events, 14.7 us)
Sparse Core Ops, SparseCore 0:
  51.2 36.5 all-gather.27
Sparse Core Ops, SparseCore 1:
  294.1 159.5 all-reduce.1
where the time goes:
time: 524 us; the launch traced here: 517 us
  blocking collectives  188 us (36%)
  waiting for transfers between devices  97.6 us (19%)
  matrix products  94 us (18%)
  local copies, waits for them, and re-layouts  58.3 us (11%)
  starting transfers between devices  43.1 us (8%)
  between operations  19.6 us (4%)
  other arithmetic  16.6 us (3%)
    all_gather x24, blocking collectives, gather_in_order(): blocks = lax.all_gather(blocks, axes[k])  188 us
    psum x1, waiting for transfers between devices, on_device(): kernel_grad = lax.psum(partial_value, FRAME_HEIGHT_WIDTH)  96.6 us
    ppermute x6, starting transfers between devices, with_halo(): lax.ppermute(tail, axis, [(i, (i + 1) % count) for i in range(ends)])  34 us
    dot_general x27, matrix products, on_device(): lax.dot_general(shifted, flat_grad, (((0,), (0,)), ((), ())), preferred_e...  34 us
    unnamed x68, local copies, waits for them, and re-layouts  21.9 us
    dot_general x1, matrix products, gram_of(): lax.dot_general(rows, rows, (((0,), (0,)), ((), ())), precision=lax.Preci...  16.8 us
    dot_general x27, matrix products, on_device(): jnp.dot(back, full_kernel[tap * chans:(tap + 1) * chans], preferred_eleme...  15 us
  transfers between devices with their start and end apart: 14, of which 2 were waited for; matrix products, arithmetic and copies ran while one was open for 19% of the time, Pallas kernels for 0%

commit v1 on v0

v1 whole, which is shorter than its diff:
```python
import functools

import jax
import jax.numpy as jnp
from jax import lax
from jax.experimental import pallas as pl
from jax.experimental.pallas import tpu as pltpu
from jax.sharding import PartitionSpec as P

MESH = pl.DeviceIdType.MESH
ITERS = 12
VMEM = pltpu.VMEM
BF = jnp.bfloat16
F32 = jnp.float32
LIMIT = 64000 * 1024
ORDERS = (("x", "y", "z"), ("y", "z", "x"), ("z", "x", "y"))
CUTS = ((0, 2), (2, 4), (4, 7))


def place():
    f, h, w = lax.axis_index("frame"), lax.axis_index("height"), lax.axis_index("width")
    return {"x": 2 * f + w % 2, "y": w // 2, "z": h // 2, "c": h % 2}


def device(at):
    return (at["x"] // 2, 2 * at["z"] + at["c"], 2 * at["y"] + at["x"] % 2)


def along(at, axis, k):
    moved = dict(at)
    moved[axis] = (at[axis] + k) % 4
    return device(moved)


def other_core(at):
    moved = dict(at)
    moved["c"] = 1 - at["c"]
    return device(moved)


def meet(partners):
    barrier = pltpu.get_barrier_semaphore()
    for partner in partners:
        pl.semaphore_signal(barrier, inc=1, device_id=partner, device_id_type=MESH)
    pl.semaphore_wait(barrier, len(partners))


def send(src, dst, sems, index, to):
    copy = pltpu.make_async_remote_copy(
        src_ref=src,
        dst_ref=dst,
        send_sem=sems[0].at[index],
        recv_sem=sems[1].at[index],
        device_id=to,
        device_id_type=MESH,
    )
    copy.start()
    return copy


def halo_kernel(g, own, gc, lc, rc, k0, k1, k2, edge, hsem, hrsem, ksem, krsem, lsem):
    at = place()
    f, h, w = lax.axis_index("frame"), lax.axis_index("height"), lax.axis_index("width")
    up, down = (f, (h + 7) % 8, w), (f, (h + 1) % 8, w)
    left, right = (f, h, (w + 7) % 8), (f, h, (w + 1) % 8)
    across = (1 - f, h, w)
    parts = (k0, k1, k2)
    hs, ks = (hsem, hrsem), (ksem, krsem)
    core = at["c"]
    index = [at[o[2]] * 16 + at[o[1]] * 4 + at[o[0]] for o in ORDERS]

    locals_ = [pltpu.make_async_copy(g, gc.at[0:4, 1:17], lsem.at[0])]
    for p, (lo, hi) in enumerate(CUTS):
        locals_.append(
            pltpu.make_async_copy(own.at[lo:hi], parts[p].at[core, index[p]], lsem.at[1 + p])
        )
    for copy in locals_:
        copy.start()
    meet(
        [up, down, left, right, across, other_core(at)]
        + [along(at, axis, k) for axis in "xyz" for k in (1, 2, 3)]
    )
    edge_frame = 3 * (1 - f)
    rows = [
        send(g.at[:, 0:1], gc.at[0:4, 17:18], hs, 0, up),
        send(g.at[:, 15:16], gc.at[0:4, 0:1], hs, 1, down),
    ]
    face = send(g.at[edge_frame], gc.at[4, 1:17], hs, 2, across)
    one = [
        send(own.at[lo:hi], parts[p].at[core, index[p]], ks, 9 * p + k - 1, along(at, ORDERS[p][0], k))
        for p, (lo, hi) in enumerate(CUTS)
        for k in (1, 2, 3)
    ]
    locals_[0].wait()
    for copy in rows:
        copy.wait_recv()
    face_rows = [
        send(gc.at[edge_frame, 0:1], gc.at[4, 0:1], hs, 3, across),
        send(gc.at[edge_frame, 17:18], gc.at[4, 17:18], hs, 4, across),
    ]
    line = lax.broadcasted_iota(jnp.int32, (64, 576), 0)
    spot = lax.broadcasted_iota(jnp.int32, (64, 576), 1)
    want = jnp.where(line < 32, line * 32 + 31, (line - 32) * 32)
    pick = jnp.where(spot == want, 1.0, 0.0).astype(BF)
    for frame in range(4):
        block = gc[frame].reshape(576, 256)
        cut = jnp.dot(pick, block, preferred_element_type=F32).astype(BF)
        edge[0, frame] = cut[:32]
        edge[1, frame] = cut[32:]
    columns = [
        send(edge.at[0], lc.at[0:4], hs, 5, right),
        send(edge.at[1], rc.at[0:4], hs, 6, left),
    ]
    for copy in locals_[1:]:
        copy.wait()
    two = []
    for p in range(3):
        for copy in one[3 * p : 3 * p + 3]:
            copy.wait_recv()
        held = parts[p].at[core, pl.ds(at[ORDERS[p][2]] * 16 + at[ORDERS[p][1]] * 4, 4)]
        two += [
            send(held, held, ks, 9 * p + 3 + k - 1, along(at, ORDERS[p][1], k)) for k in (1, 2, 3)
        ]
    for copy in columns:
        copy.wait_recv()
    face_columns = [
        send(lc.at[edge_frame], lc.at[4], hs, 7, across),
        send(rc.at[edge_frame], rc.at[4], hs, 8, across),
    ]
    three = []
    for p in range(3):
        for copy in two[3 * p : 3 * p + 3]:
            copy.wait_recv()
        held = parts[p].at[core, pl.ds(at[ORDERS[p][2]] * 16, 16)]
        three += [
            send(held, held, ks, 9 * p + 6 + k - 1, along(at, ORDERS[p][2], k)) for k in (1, 2, 3)
        ]
    pair = []
    for p in range(3):
        for copy in three[3 * p : 3 * p + 3]:
            copy.wait_recv()
        pair.append(send(parts[p].at[core], parts[p].at[core], ks, 27 + p, other_core(at)))
    for copy in [face] + face_rows + face_columns + pair:
        copy.wait_recv()
    for copy in rows + [face] + face_rows + columns + face_columns + one + two + three + pair:
        copy.wait_send()


def halo(g, own):
    return pl.pallas_call(
        halo_kernel,
        out_shape=(
            jax.ShapeDtypeStruct((5, 18, 32, 256), BF),
            jax.ShapeDtypeStruct((5, 32, 256), BF),
            jax.ShapeDtypeStruct((5, 32, 256), BF),
        )
        + tuple(jax.ShapeDtypeStruct((2, 64, hi - lo, 8, 256), BF) for lo, hi in CUTS),
        in_specs=[pl.BlockSpec(memory_space=pl.ANY)] * 2,
        out_specs=[pl.BlockSpec(memory_space=VMEM)] * 6,
        scratch_shapes=[
            VMEM((2, 4, 32, 256), BF),
            pltpu.SemaphoreType.DMA((9,)),
            pltpu.SemaphoreType.DMA((9,)),
            pltpu.SemaphoreType.DMA((30,)),
            pltpu.SemaphoreType.DMA((30,)),
            pltpu.SemaphoreType.DMA((4,)),
        ],
        compiler_params=pltpu.CompilerParams(
            collective_id=0, has_side_effects=True, vmem_limit_bytes=LIMIT
        ),
        name="halo",
    )(g, own)


def conv_kernel(act, gc, lc, rc, k0, k1, k2, kg, ig, kal, gs, lf, rf, act_t, mix):
    f, h, w = lax.axis_index("frame"), lax.axis_index("height"), lax.axis_index("width")
    lf[...] = jnp.where(w == 0, 0.0, lc[...].astype(F32))
    rf[...] = jnp.where(w == 7, 0.0, rc[...].astype(F32))
    empty = 5 * f
    sub = lax.broadcasted_iota(jnp.int32, (32, 256), 0)

    def build(r, carry):
        frame, row = r // 18, r % 18
        slot = jnp.where(frame == 4, 5 * (1 - f), frame + 1)
        off = jnp.logical_or(
            jnp.logical_and(row == 0, h == 0), jnp.logical_and(row == 17, h == 7)
        )
        keep = jnp.where(off, 0.0, 1.0)
        x = gc[frame, row].astype(F32) * keep
        before = lf[frame, pl.ds(row, 1), :] * keep
        after = rf[frame, pl.ds(row, 1), :] * keep
        gs[1, slot, row] = x.astype(BF)
        gs[0, slot, row] = jnp.where(sub == 31, after, pltpu.roll(x, 31, 0)).astype(BF)
        gs[2, slot, row] = jnp.where(sub == 0, before, pltpu.roll(x, 1, 0)).astype(BF)
        return carry

    lax.fori_loop(0, 90, build, 0)

    def clear(r, carry):
        for c in range(3):
            gs[c, empty, r] = jnp.zeros((32, 256), BF)
        return carry

    lax.fori_loop(0, 18, clear, 0)

    def align(r, carry):
        x_hi, z, c = r // 8, (r // 2) % 4, r % 2
        for col in range(8):
            spot = {"x": 2 * x_hi + col % 2, "y": col // 2, "z": z}
            for p, (part, (lo, hi)) in enumerate(zip((k0, k1, k2), CUTS)):
                o = ORDERS[p]
                block = part[c, spot[o[2]] * 16 + spot[o[1]] * 4 + spot[o[0]]].astype(F32)
                for j in range(lo, hi):
                    size = 6 if j == 6 else 8
                    mix[54 * col + 8 * j : 54 * col + 8 * j + size] = block[j - lo][:size]
        kal[pl.ds(pl.multiple_of(r * 432, 432), 432), :] = mix[...].astype(BF)
        return carry

    lax.fori_loop(0, 16, align, 0)

    for n in range(8):
        block = act[256 * n : 256 * n + 256, :].astype(F32)
        act_t[:, 256 * n : 256 * n + 256] = block.T.astype(BF)

    def weight(t, carry):
        a, b, c = t // 9, (t // 3) % 3, t % 3
        s = gs[c, pl.ds(2 - a, 4), pl.ds(2 - b, 16)].reshape(2048, 256)
        kg[t] = jnp.dot(act_t[...], s, preferred_element_type=F32)
        return carry

    lax.fori_loop(0, 27, weight, 0)

    def data(q, carry):
        taps = [
            gs[t % 3, q + 2 - t // 9, pl.ds(2 - (t // 3) % 3, 16)].reshape(512, 256)
            for t in range(27)
        ]
        total = jnp.dot(jnp.concatenate(taps, 1), kal[...], preferred_element_type=F32)
        ig[pl.ds(pl.multiple_of(q * 512, 512), 512), :] = (
            total / jnp.sqrt(jnp.float32(6912))
        ).astype(BF)
        return carry

    lax.fori_loop(0, 4, data, 0)


def conv(act, gc, lc, rc, k0, k1, k2):
    return pl.pallas_call(
        conv_kernel,
        out_shape=(
            jax.ShapeDtypeStruct((27, 256, 256), F32),
            jax.ShapeDtypeStruct((2048, 256), BF),
            jax.ShapeDtypeStruct((6912, 256), BF),
        ),
        in_specs=[pl.BlockSpec(memory_space=VMEM)] * 7,
        out_specs=[pl.BlockSpec(memory_space=VMEM)] * 3,
        scratch_shapes=[
            VMEM((3, 6, 18, 32, 256), BF),
            VMEM((5, 32, 256), F32),
            VMEM((5, 32, 256), F32),
            VMEM((256, 2048), BF),
            VMEM((432, 256), F32),
        ],
        compiler_params=pltpu.CompilerParams(vmem_limit_bytes=LIMIT),
        name="conv",
    )(act, gc, lc, rc, k0, k1, k2)


def sum_kernel(kg, f0, f1, f2, r0, s1, ra, s2, rb, s3, rc, sems, rsems):
    at = place()
    core = at["c"]
    partner = other_core(at)
    meet([partner] + [along(at, axis, k) for axis in "xyz" for k in (1, 2, 3)])
    full = (f0, f1, f2)
    pairs = (sems, rsems)
    waits = []

    def go(src, dst, index, to):
        copy = send(src, dst, pairs, index, to)
        waits.append(copy)
        return copy

    zero = [
        go(kg.at[pl.ds(9 * p, 9), pl.ds(1 - core, 1)], r0.at[pl.ds(9 * p, 9)], p, partner)
        for p in range(3)
    ]
    one = []
    for p in range(3):
        zero[p].wait_recv()

        def add(t, carry, p=p):
            s1[9 * p + t] = kg[9 * p + t, core] + r0[9 * p + t, 0]
            return carry

        lax.fori_loop(0, 9, add, 0)
        axis = ORDERS[p][0]
        for k in (1, 2, 3):
            there = (at[axis] + k) % 4
            one.append(
                go(
                    s1.at[pl.ds(9 * p, 9), pl.ds(there, 1)],
                    ra.at[p, k - 1],
                    3 + 3 * p + k - 1,
                    along(at, axis, k),
                )
            )
    two = []
    for p in range(3):
        for copy in one[3 * p : 3 * p + 3]:
            copy.wait_recv()
        mine = at[ORDERS[p][0]]

        def add(t, carry, p=p, mine=mine):
            s2[p, t] = (s1[9 * p + t, mine] + ra[p, 1, t, 0]) + (ra[p, 0, t, 0] + ra[p, 2, t, 0])
            return carry

        lax.fori_loop(0, 9, add, 0)
        axis = ORDERS[p][1]
        for k in (1, 2, 3):
            there = (at[axis] + k) % 4
            two.append(
                go(
                    s2.at[p, :, pl.ds(there, 1)],
                    rb.at[p, k - 1],
                    12 + 3 * p + k - 1,
                    along(at, axis, k),
                )
            )
    three = []
    for p in range(3):
        for copy in two[3 * p : 3 * p + 3]:
            copy.wait_recv()
        mine = at[ORDERS[p][1]]

        def add(t, carry, p=p, mine=mine):
            s3[p, t] = (s2[p, t, mine] + rb[p, 1, t, 0]) + (rb[p, 0, t, 0] + rb[p, 2, t, 0])
            return carry

        lax.fori_loop(0, 9, add, 0)
        for k in (1, 2, 3):
            three.append(
                go(s3.at[p], rc.at[p, k - 1], 21 + 3 * p + k - 1, along(at, ORDERS[p][2], k))
            )
    four = []
    for p in range(3):
        for copy in three[3 * p : 3 * p + 3]:
            copy.wait_recv()
        spot = at[ORDERS[p][0]] * 4 + at[ORDERS[p][1]]

        def add(t, carry, p=p, spot=spot):
            full[p][core, spot, t] = (s3[p, t] + rc[p, 1, t]) + (rc[p, 0, t] + rc[p, 2, t])
            return carry

        lax.fori_loop(0, 9, add, 0)
        held = full[p].at[core, pl.ds(spot, 1)]
        for k in (1, 2, 3):
            four.append(go(held, held, 30 + 3 * p + k - 1, along(at, ORDERS[p][1], k)))
    five = []
    for p in range(3):
        for copy in four[3 * p : 3 * p + 3]:
            copy.wait_recv()
        held = full[p].at[core, pl.ds(at[ORDERS[p][0]] * 4, 4)]
        for k in (1, 2, 3):
            five.append(go(held, held, 39 + 3 * p + k - 1, along(at, ORDERS[p][0], k)))
    six = []
    for p in range(3):
        for copy in five[3 * p : 3 * p + 3]:
            copy.wait_recv()
        six.append(go(full[p].at[core], full[p].at[core], 48 + p, partner))
    for copy in six:
        copy.wait_recv()
    for copy in waits:
        copy.wait_send()


def summed(kg):
    return pl.pallas_call(
        sum_kernel,
        out_shape=(jax.ShapeDtypeStruct((2, 16, 9, 8, 256), F32),) * 3,
        in_specs=[pl.BlockSpec(memory_space=VMEM)],
        out_specs=[pl.BlockSpec(memory_space=VMEM)] * 3,
        scratch_shapes=[
            VMEM((27, 1, 4, 4, 8, 256), F32),
            VMEM((27, 4, 4, 8, 256), F32),
            VMEM((3, 3, 9, 1, 4, 8, 256), F32),
            VMEM((3, 9, 4, 8, 256), F32),
            VMEM((3, 3, 9, 1, 8, 256), F32),
            VMEM((3, 9, 8, 256), F32),
            VMEM((3, 3, 9, 8, 256), F32),
            pltpu.SemaphoreType.DMA((51,)),
            pltpu.SemaphoreType.DMA((51,)),
        ],
        compiler_params=pltpu.CompilerParams(
            collective_id=1, has_side_effects=True, vmem_limit_bytes=LIMIT
        ),
        name="summed",
    )(kg)


def halves(x):
    high = x.astype(BF)
    return high, (x - high.astype(F32)).astype(BF)


def product(left, right):
    lh, ll = halves(left)
    rh, rl = halves(right)
    return jnp.dot(
        jnp.concatenate([lh, lh, ll], 1),
        jnp.concatenate([rh, rl, rh], 0),
        preferred_element_type=F32,
    )


def update_kernel(f0, f1, f2, kal, damping, out, g1, g2):
    g1[...] = jnp.zeros((256, 256), F32)
    g2[...] = jnp.zeros((256, 256), F32)
    full = (f0, f1, f2)
    for p in range(3):

        def gram(k, carry, p=p):
            high, low = halves(full[p][:, :, k].reshape(256, 256))
            turned = high.astype(F32).T.astype(BF)
            g1[...] += jnp.dot(turned, high, preferred_element_type=F32)
            g2[...] += jnp.dot(turned, low, preferred_element_type=F32)
            return carry

        lax.fori_loop(0, 9, gram, 0)
    cross = g2[...]
    total = g1[...] + (cross + cross.T)
    row = lax.broadcasted_iota(jnp.int32, (256, 256), 0)
    column = lax.broadcasted_iota(jnp.int32, (256, 256), 1)
    identity = jnp.where(row == column, 1.0, 0.0).astype(F32)

    def whole(x):
        return jnp.sum(jnp.sum(x, axis=1, keepdims=True), axis=0, keepdims=True)

    factor = total + (damping[0, 0] / 256.0) * whole(total * identity) * identity
    scale = 2.5 / jnp.sqrt(whole(factor * factor))
    root = jnp.sqrt(jnp.sqrt(scale)) * identity
    matrix = scale * factor

    def newton(step, carry):
        root, matrix = carry
        middle = (5.0 * identity - matrix) / 4.0
        root = product(root, middle)
        square = product(middle, middle)
        return root, product(square, product(square, matrix))

    root, matrix = lax.fori_loop(0, ITERS, newton, (root, matrix))
    energy = whole(root * product(total, root))
    size = jnp.sqrt(energy / (6912.0 * 256.0) + 1e-6)
    rate = 0.5 / size
    rh, rl = halves(root)
    stack = jnp.concatenate([rh, rl, rh], 0)
    for p in range(3):

        def write(k, carry, p=p):
            high, low = halves(full[p][:, :, k].reshape(256, 256))
            direction = jnp.dot(
                jnp.concatenate([high, high, low], 1), stack, preferred_element_type=F32
            )
            rows = pl.ds(pl.multiple_of((9 * p + k) * 256, 256), 256)
            out[rows, :] = (kal[rows, :].astype(F32) - rate * direction).astype(BF)
            return carry

        lax.fori_loop(0, 9, write, 0)


def update(f0, f1, f2, kal, damping):
    return pl.pallas_call(
        update_kernel,
        out_shape=jax.ShapeDtypeStruct((6912, 256), BF),
        in_specs=[pl.BlockSpec(memory_space=VMEM)] * 4 + [pl.BlockSpec(memory_space=pltpu.SMEM)],
        out_specs=pl.BlockSpec(memory_space=VMEM),
        scratch_shapes=[VMEM((256, 256), F32), VMEM((256, 256), F32)],
        compiler_params=pltpu.CompilerParams(vmem_limit_bytes=LIMIT),
        name="update",
    )(f0, f1, f2, kal, damping)


def on_device(activations, out_grad, kernel, damping):
    own = jnp.pad(kernel, ((0, 2), (0, 0))).reshape(7, 8, 256)
    gc, lc, rc, k0, k1, k2 = halo(out_grad, own)
    kg, ig, kal = conv(activations.reshape(2048, 256), gc, lc, rc, k0, k1, k2)
    f0, f1, f2 = summed(kg.reshape(27, 2, 4, 4, 8, 256))
    new_kernel = update(f0, f1, f2, kal, damping.reshape(1, 1))
    return ig.reshape(activations.shape), new_kernel


def solution(mesh):
    placed = (
        P("frame", "height", "width", None),
        P("frame", "height", "width", None),
        P(("frame", "height", "width"), None),
        P(),
    )
    return jax.shard_map(
        on_device,
        mesh=mesh,
        in_specs=placed,
        out_specs=(P("frame", "height", "width", None), P()),
        check_vma=False,
    )
```

time: 524 us -> 169 us (0.32); the launches traced: 517 us -> 169 us
  blocking collectives: 188 us -> 0 us
  Pallas kernels: 0 us -> 166 us
  waiting for transfers between devices: 97.6 us -> 0 us
  matrix products: 94 us -> 0 us
  local copies, waits for them, and re-layouts: 58.3 us -> 1.36 us
  starting transfers between devices: 43.1 us -> 0 us
  between operations: 19.6 us -> 1.29 us
  other arithmetic: 16.6 us -> 0 us
    all_gather x24 -> x0, blocking collectives: 188 us -> none  [gather_in_order(): blocks = lax.all_gather(blocks, axes[k])]
    pallas_call x0 -> x4, Pallas kernels: none -> 166 us  [the longest x1 65.8 us: summed(): pl.pallas_call(sum_kernel, out_shape=(jax.ShapeDtypeStruct((2, 16, 9, 8,...]
    psum x1 -> x0, waiting for transfers between devices: 96.6 us -> none  [on_device(): kernel_grad = lax.psum(partial_value, FRAME_HEIGHT_WIDTH)]
    dot_general x101 -> x0, matrix products: 94 us -> none  [the longest x27 34 us: on_device(): lax.dot_general(shifted, flat_grad, (((0,), (0,)), ((), ())), preferred_e...]
    ppermute x12 -> x0, starting transfers between devices: 43 us -> none  [the longest x6 34 us: with_halo(): lax.ppermute(tail, axis, [(i, (i + 1) % count) for i in range(ends)])]
    unnamed x68 -> x0, local copies, waits for them, and re-layouts: 21.9 us -> none
    slice x5 -> x0, local copies, waits for them, and re-layouts: 10.9 us -> none  [the longest x1 8.14 us: on_device(): padded_grad[2 - tap_f:2 - tap_f + frames, 2 - tap_h:2 - tap_h + height, 2...]
    reshape x5 -> x1, local copies, waits for them, and re-layouts: 10.6 us -> 1.36 us  [on_device(): own = jnp.pad(kernel, ((0, 2), (0, 0))).reshape(7, 8, 256)]
  transfers between devices with their start and end apart: 14 -> 0, of which waited for: 2 -> 0; matrix products, arithmetic and copies ran while one was open for 19% -> 0% of each run, Pallas kernels for 0% -> 0%
where the time goes in v1:
time: 169 us
  Pallas kernels  166 us (98%)
    pallas_call x1, Pallas kernels, summed(): pl.pallas_call(sum_kernel, out_shape=(jax.ShapeDtypeStruct((2, 16, 9, 8,...  65.8 us
    pallas_call x1, Pallas kernels, halo(): pl.pallas_call(halo_kernel, out_shape=(jax.ShapeDtypeStruct((5, 18, 32, 2...  37 us
    pallas_call x1, Pallas kernels, update(): pl.pallas_call(update_kernel, out_shape=jax.ShapeDtypeStruct((6912, 256),...  33.5 us
    pallas_call x1, Pallas kernels, conv(): pl.pallas_call(conv_kernel, out_shape=(jax.ShapeDtypeStruct((27, 256, 256...  29.6 us

profile of v1, /device:TPU:1, one launch (start us, length us, event | category | flops | bytes accessed | tf_op | source)
XLA Modules:
  0.0 168.5 jit_solution(13094127426952464740)
XLA Ops:
  0.6 1.4 pad_bitcast_fusion.own
  2.0 37.0 %halo.1 = (bf16[5,18,32,256]{3,2,1,0:T(8,128)(2,1)}, bf16[5,32,256]{2,1,0:T(8,128)(2,1)}, bf16[5,32,256]{2,1,0:T(8,128)(2,1)}, bf16[2,64,2,8,256]{4,3,2,1,0:T(8,...) custom-call(bf16[4,16,32,256]{3,2,1,0:T(8,128)(2,1)} %g.1, ...), custom_call_target="tpu_custom_call" | custom-call | tf_op jit(solution)/shard_map/halo/pallas_call | solution.py:150
  39.0 29.6 %conv.1 = (f32[27,256,256]{2,1,0:T(8,128)}, bf16[2048,256]{1,0:T(8,128)(2,1)}, bf16[6912,256]{1,0:T(8,128)(2,1)}) custom-call(bf16[2048,256]{1,0:T(8,128)(2,1)} %bitcast.8, bf16[5,18,32,256]{3,2,1,0:T(8,128)(2,1)} %get-tuple-element.14.gc, bf16[5,32,256]{2,1,0:T(8,128)(2,1)} %get-tuple-element.15.lc, bf16[5,32,256]{2,1,0:T(8,128)(2,1)} %get-tuple-element.16.rc, ...), custom_call_target="tpu_custom_call" | custom-call | tf_op jit(solution)/shard_map/conv/pallas_call | solution.py:248
  68.6 65.8 %summed.1 = (f32[2,16,9,8,256]{4,3,2,1,0:T(8,128)}, f32[2,16,9,8,256]{4,3,2,1,0:T(8,128)}, f32[2,16,9,8,256]{4,3,2,1,0:T(8,128)}) custom-call(f32[27,2,4,4,8,256]{5,4,3,2,1,0:T(8,128)} %bitcast.7), custom_call_target="tpu_custom_call" | custom-call | tf_op jit(solution)/shard_map/summed/pallas_call | solution.py:377
  135.0 33.5 %update.1 = bf16[6912,256]{1,0:T(8,128)(2,1)} custom-call(f32[2,16,9,8,256]{4,3,2,1,0:T(8,128)} %get-tuple-element.22.f0, f32[2,16,9,8,256]{4,3,2,1,0:T(8,128)} %get-tuple-element.23.f1, f32[2,16,9,8,256]{4,3,2,1,0:T(8,128)} %get-tuple-element.24.f2, bf16[6912,256]{1,0:T(8,128)(2,1)} %get-tuple-element.25.kal, f32[1,1]{1,0:T(1,128)} %bitcast.6.damping), custom_call_target="tpu_custom_call" | custom-call | tf_op jit(solution)/shard_map/update/pallas_call | solution.py:471

commit v2 on v0

v2 whole, which is shorter than its diff:
```python
import functools

import jax
import jax.numpy as jnp
from jax import lax
from jax.experimental import pallas as pl
from jax.experimental.pallas import tpu as pltpu
from jax.sharding import PartitionSpec as P

MESH = pl.DeviceIdType.MESH
ITERS = 12
VMEM = pltpu.VMEM
BF = jnp.bfloat16
F32 = jnp.float32
LIMIT = 65000 * 1024
ORDERS = (("x", "y", "z"), ("y", "z", "x"), ("z", "x", "y"))
CUTS = ((0, 2), (2, 4), (4, 7))


def place():
    f, h, w = lax.axis_index("frame"), lax.axis_index("height"), lax.axis_index("width")
    return {"x": 2 * f + w % 2, "y": w // 2, "z": h // 2, "c": h % 2}


def device(at):
    return (at["x"] // 2, 2 * at["z"] + at["c"], 2 * at["y"] + at["x"] % 2)


def along(at, axis, k):
    moved = dict(at)
    moved[axis] = (at[axis] + k) % 4
    return device(moved)


def other_core(at):
    moved = dict(at)
    moved["c"] = 1 - at["c"]
    return device(moved)


def meet(partners):
    barrier = pltpu.get_barrier_semaphore()
    for partner in partners:
        pl.semaphore_signal(barrier, inc=1, device_id=partner, device_id_type=MESH)
    pl.semaphore_wait(barrier, len(partners))


def send(src, dst, sems, index, to):
    copy = pltpu.make_async_remote_copy(
        src_ref=src,
        dst_ref=dst,
        send_sem=sems[0].at[index],
        recv_sem=sems[1].at[index],
        device_id=to,
        device_id_type=MESH,
    )
    copy.start()
    return copy


def halves(x):
    high = x.astype(BF)
    return high, (x - high.astype(F32)).astype(BF)


def product(left, right):
    lh, ll = halves(left)
    rh, rl = halves(right)
    return jnp.dot(
        jnp.concatenate([lh, lh, ll], 1),
        jnp.concatenate([rh, rl, rh], 0),
        preferred_element_type=F32,
    )


def whole(x):
    return jnp.sum(jnp.sum(x, axis=1, keepdims=True), axis=0, keepdims=True)


N_SENDS = 9 + 30 + 51 + 11 + 27
SCRATCH = dict(
    gc=VMEM((5, 18, 32, 256), BF),
    lc=VMEM((5, 32, 256), BF),
    rc=VMEM((5, 32, 256), BF),
    edge=VMEM((2, 4, 32, 256), BF),
    k0=VMEM((2, 64, 2, 8, 256), BF),
    k1=VMEM((2, 64, 2, 8, 256), BF),
    k2=VMEM((2, 64, 3, 8, 256), BF),
    gs=VMEM((3, 6, 18, 32, 256), BF),
    lf=VMEM((5, 32, 256), F32),
    rf=VMEM((5, 32, 256), F32),
    act_t=VMEM((256, 2048), BF),
    mix=VMEM((432, 256), F32),
    kal=VMEM((6912, 256), BF),
    kg=VMEM((27, 2, 4, 4, 8, 256), F32),
    r0=VMEM((27, 1, 4, 4, 8, 256), F32),
    s1=VMEM((27, 4, 4, 8, 256), F32),
    ra=VMEM((3, 3, 9, 1, 4, 8, 256), F32),
    s2=VMEM((3, 9, 4, 8, 256), F32),
    rb=VMEM((3, 3, 9, 1, 8, 256), F32),
    s3=VMEM((3, 9, 8, 256), F32),
    r3=VMEM((3, 3, 9, 8, 256), F32),
    f0=VMEM((2, 16, 9, 8, 256), F32),
    f1=VMEM((2, 16, 9, 8, 256), F32),
    f2=VMEM((2, 16, 9, 8, 256), F32),
    gp=VMEM((3, 2, 64, 128), F32),
    gr0=VMEM((3, 64, 128), F32),
    ga=VMEM((3, 3, 64, 128), F32),
    gr=VMEM((3, 3, 3, 64, 128), F32),
    gfull=VMEM((2, 3, 64, 128), F32),
    total=VMEM((256, 256), F32),
    root=VMEM((256, 256), F32),
    matrix=VMEM((256, 256), F32),
    sems=pltpu.SemaphoreType.DMA((N_SENDS,)),
    rsems=pltpu.SemaphoreType.DMA((N_SENDS,)),
    lsem=pltpu.SemaphoreType.DMA((4,)),
)


class Refs:
    pass


def step_kernel(g, own, act, damping, ig, out, *scratch):
    r = Refs()
    for name, ref in zip(SCRATCH, scratch):
        setattr(r, name, ref)
    at = place()
    f, h, w = lax.axis_index("frame"), lax.axis_index("height"), lax.axis_index("width")
    up, down = (f, (h + 7) % 8, w), (f, (h + 1) % 8, w)
    left, right = (f, h, (w + 7) % 8), (f, h, (w + 1) % 8)
    across = (1 - f, h, w)
    core = at["c"]
    partner = other_core(at)
    parts, full = (r.k0, r.k1, r.k2), (r.f0, r.f1, r.f2)
    mine = [[at[axis] for axis in o] for o in ORDERS]
    sent = []

    def go(src, dst, to):
        copy = send(src, dst, (r.sems, r.rsems), len(sent), to)
        sent.append(copy)
        return copy

    def three(src, dst, p, s):
        return [go(src(k), dst(k), along(at, ORDERS[p][s], k)) for k in (1, 2, 3)]

    def landed(copies):
        for copy in copies:
            copy.wait_recv()

    index = [m[2] * 16 + m[1] * 4 + m[0] for m in mine]
    here = [pltpu.make_async_copy(g, r.gc.at[0:4, 1:17], r.lsem.at[0])]
    for p, (lo, hi) in enumerate(CUTS):
        here.append(
            pltpu.make_async_copy(own.at[lo:hi], parts[p].at[core, index[p]], r.lsem.at[1 + p])
        )
    for copy in here:
        copy.start()
    meet(
        [up, down, left, right, across, partner]
        + [along(at, axis, k) for axis in "xyz" for k in (1, 2, 3)]
    )
    last = 3 * (1 - f)
    rows = [
        go(g.at[:, 0:1], r.gc.at[0:4, 17:18], up),
        go(g.at[:, 15:16], r.gc.at[0:4, 0:1], down),
    ]
    face = [go(g.at[last], r.gc.at[4, 1:17], across)]
    gather = [
        three(lambda k: own.at[lo:hi], lambda k: parts[p].at[core, index[p]], p, 0)
        for p, (lo, hi) in enumerate(CUTS)
    ]
    for n in range(8):
        block = act[256 * n : 256 * n + 256, :].astype(F32)
        r.act_t[:, 256 * n : 256 * n + 256] = block.T.astype(BF)
    line = lax.broadcasted_iota(jnp.int32, (64, 576), 0)
    spot = lax.broadcasted_iota(jnp.int32, (64, 576), 1)
    want = jnp.where(line < 32, line * 32 + 31, (line - 32) * 32)
    pick = jnp.where(spot == want, 1.0, 0.0).astype(BF)
    here[0].wait()
    landed(rows)
    face += [
        go(r.gc.at[last, 0:1], r.gc.at[4, 0:1], across),
        go(r.gc.at[last, 17:18], r.gc.at[4, 17:18], across),
    ]
    for frame in range(4):
        block = r.gc[frame].reshape(576, 256)
        cut = jnp.dot(pick, block, preferred_element_type=F32).astype(BF)
        r.edge[0, frame] = cut[:32]
        r.edge[1, frame] = cut[32:]
    columns = [
        go(r.edge.at[0], r.lc.at[0:4], right),
        go(r.edge.at[1], r.rc.at[0:4], left),
    ]
    for copy in here[1:]:
        copy.wait()
    for p in range(3):
        landed(gather[p])
        held = parts[p].at[core, pl.ds(mine[p][2] * 16 + mine[p][1] * 4, 4)]
        gather[p] = three(lambda k: held, lambda k: held, p, 1)
    landed(columns)
    face += [
        go(r.lc.at[last], r.lc.at[4], across),
        go(r.rc.at[last], r.rc.at[4], across),
    ]

    sub = lax.broadcasted_iota(jnp.int32, (32, 256), 0)

    def build(n, carry):
        frame, row = n // 18, n % 18
        slot = jnp.where(frame == 4, 5 * (1 - f), frame + 1)
        off = jnp.logical_or(
            jnp.logical_and(row == 0, h == 0), jnp.logical_and(row == 17, h == 7)
        )
        keep = jnp.where(off, 0.0, 1.0)
        x = r.gc[frame, row].astype(F32) * keep
        before = r.lf[frame, pl.ds(row, 1), :] * keep
        after = r.rf[frame, pl.ds(row, 1), :] * keep
        r.gs[1, slot, row] = x.astype(BF)
        r.gs[0, slot, row] = jnp.where(sub == 31, after, pltpu.roll(x, 31, 0)).astype(BF)
        r.gs[2, slot, row] = jnp.where(sub == 0, before, pltpu.roll(x, 1, 0)).astype(BF)
        return carry

    def clear(n, carry):
        for c in range(3):
            r.gs[c, 5 * f, n] = jnp.zeros((32, 256), BF)
        return carry

    r.lf[0:4] = jnp.where(w == 0, 0.0, r.lc[0:4].astype(F32))
    r.rf[0:4] = jnp.where(w == 7, 0.0, r.rc[0:4].astype(F32))
    lax.fori_loop(0, 72, build, 0)
    lax.fori_loop(0, 18, clear, 0)
    for p in range(3):
        landed(gather[p])
        held = parts[p].at[core, pl.ds(mine[p][2] * 16, 16)]
        gather[p] = three(lambda k: held, lambda k: held, p, 2)

    def weight(t, carry):
        a, b, c = t // 9, (t // 3) % 3, t % 3
        s = r.gs[c, pl.ds(2 - a, 4), pl.ds(2 - b, 16)].reshape(2048, 256)
        r.kg[t] = jnp.dot(r.act_t[...], s, preferred_element_type=F32).reshape(2, 4, 4, 8, 256)
        return carry

    def swap(p):
        lax.fori_loop(9 * p, 9 * p + 9, weight, 0)
        rows = pl.ds(9 * p, 9)
        return go(r.kg.at[rows, pl.ds(1 - core, 1)], r.r0.at[rows], partner)

    def first(p, copy):
        copy.wait_recv()

        def add(t, carry):
            r.s1[t] = r.kg[t, core] + r.r0[t, 0]
            return carry

        lax.fori_loop(9 * p, 9 * p + 9, add, 0)
        rows = pl.ds(9 * p, 9)
        return three(
            lambda k: r.s1.at[rows, pl.ds((mine[p][0] + k) % 4, 1)],
            lambda k: r.ra.at[p, k - 1],
            p,
            0,
        )

    parted = [None] * 3
    swap1 = swap(1)
    landed(face)
    r.lf[4] = jnp.where(w == 0, 0.0, r.lc[4].astype(F32))
    r.rf[4] = jnp.where(w == 7, 0.0, r.rc[4].astype(F32))
    lax.fori_loop(72, 90, build, 0)
    swap0 = swap(0)
    parted[1] = first(1, swap1)
    swap2 = swap(2)
    parted[0] = first(0, swap0)
    for p in range(3):
        landed(gather[p])
        gather[p] = [go(parts[p].at[core], parts[p].at[core], partner)]
    parted[2] = first(2, swap2)

    def align(n, carry):
        x_hi, z, c = n // 8, (n // 2) % 4, n % 2
        for col in range(8):
            spot = {"x": 2 * x_hi + col % 2, "y": col // 2, "z": z}
            for p, (part, (lo, hi)) in enumerate(zip(parts, CUTS)):
                o = ORDERS[p]
                block = part[c, spot[o[2]] * 16 + spot[o[1]] * 4 + spot[o[0]]].astype(F32)
                for j in range(lo, hi):
                    size = 6 if j == 6 else 8
                    r.mix[54 * col + 8 * j : 54 * col + 8 * j + size] = block[j - lo][:size]
        r.kal[pl.ds(pl.multiple_of(n * 432, 432), 432), :] = r.mix[...].astype(BF)
        return carry

    def data(q, carry):
        taps = [
            r.gs[t % 3, q + 2 - t // 9, pl.ds(2 - (t // 3) % 3, 16)].reshape(512, 256)
            for t in range(27)
        ]
        sums = jnp.dot(jnp.concatenate(taps, 1), r.kal[...], preferred_element_type=F32)
        ig[pl.ds(pl.multiple_of(q * 512, 512), 512), :] = (
            sums / jnp.sqrt(jnp.float32(6912))
        ).astype(BF)
        return carry

    for p in range(3):
        landed(gather[p])
    lax.fori_loop(0, 16, align, 0)
    lax.fori_loop(0, 4, data, 0)

    for p in (1, 0, 2):
        landed(parted[p])

        def add(t, carry, p=p):
            r.s2[p, t] = (r.s1[9 * p + t, mine[p][0]] + r.ra[p, 1, t, 0]) + (
                r.ra[p, 0, t, 0] + r.ra[p, 2, t, 0]
            )
            return carry

        lax.fori_loop(0, 9, add, 0)
        parted[p] = three(
            lambda k: r.s2.at[p, :, pl.ds((mine[p][1] + k) % 4, 1)],
            lambda k: r.rb.at[p, k - 1],
            p,
            1,
        )
    for p in (1, 0, 2):
        landed(parted[p])

        def add(t, carry, p=p):
            r.s3[p, t] = (r.s2[p, t, mine[p][1]] + r.rb[p, 1, t, 0]) + (
                r.rb[p, 0, t, 0] + r.rb[p, 2, t, 0]
            )
            return carry

        lax.fori_loop(0, 9, add, 0)
        parted[p] = three(lambda k: r.s3.at[p], lambda k: r.r3.at[p, k - 1], p, 2)
    spots = [m[0] * 4 + m[1] for m in mine]
    for p in (1, 0, 2):
        landed(parted[p])

        def add(t, carry, p=p):
            full[p][core, spots[p], t] = (r.s3[p, t] + r.r3[p, 1, t]) + (
                r.r3[p, 0, t] + r.r3[p, 2, t]
            )
            return carry

        lax.fori_loop(0, 9, add, 0)

    x = jnp.concatenate([full[p][core, spots[p]].reshape(72, 256) for p in range(3)], 0)
    gram = 0.25 * lax.dot_general(
        x, x, (((0,), (0,)), ((), ())), precision=lax.Precision.HIGHEST, preferred_element_type=F32
    )
    for p, block in enumerate((gram[:128, :128], gram[:128, 128:], gram[128:, 128:])):
        r.gp[p] = block.reshape(2, 64, 128)
    halfgram = go(r.gp.at[:, 1 - core], r.gr0, partner)
    spread = []
    for p in range(3):
        held = full[p].at[core, pl.ds(spots[p], 1)]
        spread.append(three(lambda k: held, lambda k: held, p, 1))
    halfgram.wait_recv()
    r.ga[0] = r.gp[:, core] + r.gr0[...]
    for s in range(3):
        hops = [
            three(lambda k: r.ga.at[s, p], lambda k: r.gr.at[s, p, k - 1], p, s) for p in range(3)
        ]
        for p in range(3):
            landed(hops[p])
            value = (r.ga[s, p] + r.gr[s, p, 1]) + (r.gr[s, p, 0] + r.gr[s, p, 2])
            if s < 2:
                r.ga[s + 1, p] = value
            else:
                r.gfull[core, p] = value
    other = go(r.gfull.at[core], r.gfull.at[core], partner)
    for p in range(3):
        landed(spread[p])
        held = full[p].at[core, pl.ds(mine[p][0] * 4, 4)]
        spread[p] = three(lambda k: held, lambda k: held, p, 0)
    other.wait_recv()
    b0, b1, b2 = [r.gfull[:, p].reshape(128, 128) for p in range(3)]
    r.total[...] = jnp.concatenate(
        [jnp.concatenate([b0, b1], 1), jnp.concatenate([b1.T, b2], 1)], 0
    )

    row = lax.broadcasted_iota(jnp.int32, (256, 256), 0)
    column = lax.broadcasted_iota(jnp.int32, (256, 256), 1)
    identity = jnp.where(row == column, 1.0, 0.0).astype(F32)
    factor = r.total[...] + (damping[0, 0] / 256.0) * whole(r.total[...] * identity) * identity
    scale = 2.5 / jnp.sqrt(whole(factor * factor))
    r.root[...] = jnp.sqrt(jnp.sqrt(scale)) * identity
    r.matrix[...] = scale * factor

    def newton(n, carry):
        middle = (5.0 * identity - r.matrix[...]) / 4.0
        both = product(jnp.concatenate([r.root[...], middle], 0), middle)
        r.root[...] = both[:256]
        square = both[256:]
        r.matrix[...] = product(square, product(square, r.matrix[...]))
        return carry

    lax.fori_loop(0, ITERS - 3, newton, 0)
    for p in range(3):
        landed(spread[p])
        spread[p] = [go(full[p].at[core], full[p].at[core], partner)]
    lax.fori_loop(ITERS - 3, ITERS, newton, 0)
    root = r.root[...]
    energy = whole(root * product(r.total[...], root))
    size = jnp.sqrt(energy / (6912.0 * 256.0) + 1e-6)
    rate = 0.5 / size
    rh, rl = halves(root)
    stack = jnp.concatenate([rh, rl, rh], 0)
    for p in range(3):
        landed(spread[p])

        def write(k, carry, p=p):
            high, low = halves(full[p][:, :, k].reshape(256, 256))
            direction = jnp.dot(
                jnp.concatenate([high, high, low], 1), stack, preferred_element_type=F32
            )
            lines = pl.ds(pl.multiple_of((9 * p + k) * 256, 256), 256)
            out[lines, :] = (r.kal[lines, :].astype(F32) - rate * direction).astype(BF)
            return carry

        lax.fori_loop(0, 9, write, 0)
    for copy in sent:
        copy.wait_send()
    assert len(sent) <= N_SENDS, len(sent)


def step(g, own, act, damping):
    return pl.pallas_call(
        step_kernel,
        out_shape=(
            jax.ShapeDtypeStruct((2048, 256), BF),
            jax.ShapeDtypeStruct((6912, 256), BF),
        ),
        in_specs=[
            pl.BlockSpec(memory_space=pl.ANY),
            pl.BlockSpec(memory_space=pl.ANY),
            pl.BlockSpec(memory_space=VMEM),
            pl.BlockSpec(memory_space=pltpu.SMEM),
        ],
        out_specs=[pl.BlockSpec(memory_space=VMEM)] * 2,
        scratch_shapes=list(SCRATCH.values()),
        compiler_params=pltpu.CompilerParams(
            collective_id=0, has_side_effects=True, vmem_limit_bytes=LIMIT
        ),
        name="step",
    )(g, own, act, damping)


def on_device(activations, out_grad, kernel, damping):
    own = jnp.pad(kernel, ((0, 2), (0, 0))).reshape(7, 8, 256)
    ig, new_kernel = step(
        out_grad, own, activations.reshape(2048, 256), damping.reshape(1, 1)
    )
    return ig.reshape(activations.shape), new_kernel


def solution(mesh):
    placed = (
        P("frame", "height", "width", None),
        P("frame", "height", "width", None),
        P(("frame", "height", "width"), None),
        P(),
    )
    return jax.shard_map(
        on_device,
        mesh=mesh,
        in_specs=placed,
        out_specs=(P("frame", "height", "width", None), P()),
        check_vma=False,
    )
```

time: 524 us -> 119 us (0.23); the launches traced: 517 us -> 119 us
  blocking collectives: 188 us -> 0 us
  Pallas kernels: 0 us -> 110 us
  waiting for transfers between devices: 97.6 us -> 0 us
  matrix products: 94 us -> 0 us
  local copies, waits for them, and re-layouts: 58.3 us -> 7.65 us
  starting transfers between devices: 43.1 us -> 0 us
  between operations: 19.6 us -> 1.29 us
  other arithmetic: 16.6 us -> 0 us
    all_gather x24 -> x0, blocking collectives: 188 us -> none  [gather_in_order(): blocks = lax.all_gather(blocks, axes[k])]
    pallas_call x0 -> x1, Pallas kernels: none -> 110 us  [step(): pl.pallas_call(step_kernel, out_shape=(jax.ShapeDtypeStruct((2048, 256),...]
    psum x1 -> x0, waiting for transfers between devices: 96.6 us -> none  [on_device(): kernel_grad = lax.psum(partial_value, FRAME_HEIGHT_WIDTH)]
    dot_general x101 -> x0, matrix products: 94 us -> none  [the longest x27 34 us: on_device(): lax.dot_general(shifted, flat_grad, (((0,), (0,)), ((), ())), preferred_e...]
    ppermute x12 -> x0, starting transfers between devices: 43 us -> none  [the longest x6 34 us: with_halo(): lax.ppermute(tail, axis, [(i, (i + 1) % count) for i in range(ends)])]
    unnamed x68 -> x2, local copies, waits for them, and re-layouts: 21.9 us -> 6.28 us
    slice x5 -> x0, local copies, waits for them, and re-layouts: 10.9 us -> none  [the longest x1 8.14 us: on_device(): padded_grad[2 - tap_f:2 - tap_f + frames, 2 - tap_h:2 - tap_h + height, 2...]
    reshape x5 -> x1, local copies, waits for them, and re-layouts: 10.6 us -> 1.36 us  [on_device(): own = jnp.pad(kernel, ((0, 2), (0, 0))).reshape(7, 8, 256)]
  transfers between devices with their start and end apart: 14 -> 0, of which waited for: 2 -> 0; matrix products, arithmetic and copies ran while one was open for 19% -> 0% of each run, Pallas kernels for 0% -> 0%
where the time goes in v2:
time: 119 us
  Pallas kernels  110 us (92%)
  local copies, waits for them, and re-layouts  7.65 us (6%)
  between operations  1.29 us (1%)
    pallas_call x1, Pallas kernels, step(): pl.pallas_call(step_kernel, out_shape=(jax.ShapeDtypeStruct((2048, 256),...  110 us
    unnamed x2, local copies, waits for them, and re-layouts  6.28 us

profile of v2, /device:TPU:1, one launch (start us, length us, event | category | flops | bytes accessed | tf_op | source)
XLA Modules:
  0.0 119.1 jit_solution(14715275589806940438)
XLA Ops:
  1.3 1.4 %pad_bitcast_fusion.own = bf16[7,8,256]{2,1,0:T(8,128)(2,1)} fusion(bf16[54,256]{1,0:T(8,128)(2,1)} %param.6), kind=kLoop, calls=%fused_computation | loop fusion | bytes 56320 | tf_op jit(solution)/shard_map/reshape | solution.py:451
  2.6 110.1 %step.1 = (bf16[2048,256]{1,0:T(8,128)(2,1)}, bf16[6912,256]{1,0:T(8,128)(2,1)}) custom-call(bf16[4,16,32,256]{3,2,1,0:T(8,128)(2,1)} %g.1, bf16[7,8,256]{2,1,0:T(8,128)(2,1)} %pad_bitcast_fusion.own, bf16[2048,256]{1,0:T(8,128)(2,1)} %bitcast.6, f32[1,1]{1,0:T(1,128)} %bitcast.5.damping), custom_call_target="tpu_custom_call" | custom-call | tf_op jit(solution)/shard_map/step/pallas_call | solution.py:429
  112.8 2.3 %copy.9 = bf16[4,16,32,256]{3,2,1,0:T(8,128)(2,1)} copy(bf16[4,16,32,256]{3,2,1,0:T(8,128)(2,1)} %bitcast.7) | data formatting | bytes 2097152
  115.1 4.0 %copy.10 = bf16[6912,256]{1,0:T(8,128)(2,1)} copy(bf16[6912,256]{1,0:T(8,128)(2,1)} %get-tuple-element.9) | data formatting | bytes 7077888

commit v3 on v2

v3 whole, which is shorter than its diff:
```python
import functools

import jax
import jax.numpy as jnp
from jax import lax
from jax.experimental import pallas as pl
from jax.experimental.pallas import tpu as pltpu
from jax.sharding import PartitionSpec as P

MESH = pl.DeviceIdType.MESH
ITERS = 12
ON, OVER = 4, 8
VMEM = pltpu.VMEM
BF = jnp.bfloat16
F32 = jnp.float32
LIMIT = 51 * 1024 * 1024
ORDERS = (("x", "y", "z"), ("y", "z", "x"), ("z", "x", "y"))
CUTS = ((0, 16), (16, 32), (32, 54))


def place():
    f, h, w = lax.axis_index("frame"), lax.axis_index("height"), lax.axis_index("width")
    return {"x": 2 * f + w % 2, "y": w // 2, "z": h // 2, "c": h % 2}


def device(at):
    return (at["x"] // 2, 2 * at["z"] + at["c"], 2 * at["y"] + at["x"] % 2)


def along(at, axis, k):
    moved = dict(at)
    moved[axis] = (at[axis] + k) % 4
    return device(moved)


def turn(at, b, s):
    which = (b + s) % 3
    return jnp.where(which == 0, at["x"], jnp.where(which == 1, at["y"], at["z"]))


def turned(at, b, s, k):
    which, moved = (b + s) % 3, dict(at)
    for n, axis in enumerate("xyz"):
        moved[axis] = jnp.where(which == n, (at[axis] + k) % 4, at[axis])
    return device(moved)


def other_core(at):
    moved = dict(at)
    moved["c"] = 1 - at["c"]
    return device(moved)


def meet(partners):
    barrier = pltpu.get_barrier_semaphore()
    for partner in partners:
        pl.semaphore_signal(barrier, inc=1, device_id=partner, device_id_type=MESH)
    pl.semaphore_wait(barrier, len(partners))


def halves(x):
    high = x.astype(BF)
    return high, (x - high.astype(F32)).astype(BF)


def product(left, right):
    lh, ll = halves(left)
    rh, rl = halves(right)
    return jnp.dot(
        jnp.concatenate([lh, lh, ll], 1),
        jnp.concatenate([rh, rl, rh], 0),
        preferred_element_type=F32,
    )


def whole(x):
    return jnp.sum(jnp.sum(x, axis=1, keepdims=True), axis=0, keepdims=True)


N_SENDS = 110
SCRATCH = dict(
    gc=VMEM((5, 18, 32, 256), BF),
    act=VMEM((2048, 256), BF),
    ownv=VMEM((54, 256), BF),
    o0=VMEM((16, 256), BF),
    o1=VMEM((16, 256), BF),
    o2=VMEM((24, 256), BF),
    lc=VMEM((5, 16, 256), BF),
    rc=VMEM((5, 16, 256), BF),
    edge=VMEM((2, 4, 16, 256), BF),
    spots=VMEM((4, 16, 256), F32),
    cs=VMEM((4, 16, 256), BF),
    cr=VMEM((4, 16, 256), BF),
    cf=VMEM((4, 16, 256), BF),
    k0=VMEM((2, 64, 16, 256), BF),
    k1=VMEM((2, 64, 16, 256), BF),
    k2=VMEM((2, 64, 24, 256), BF),
    gs=VMEM((3, 6, 18, 32, 256), BF),
    lf=VMEM((5, 18, 256), F32),
    rf=VMEM((5, 18, 256), F32),
    act_t=VMEM((256, 2048), BF),
    mix=VMEM((432, 256), F32),
    kal=VMEM((6912, 256), BF),
    kg=VMEM((9, 3, 2, 4, 4, 8, 256), F32),
    r0=VMEM((9, 3, 1, 4, 4, 8, 256), F32),
    s1=VMEM((9, 3, 4, 4, 8, 256), F32),
    ra=VMEM((9, 3, 3, 1, 4, 8, 256), F32),
    s2=VMEM((9, 3, 4, 8, 256), F32),
    rb=VMEM((9, 3, 3, 1, 8, 256), F32),
    s3=VMEM((9, 3, 8, 256), F32),
    r3=VMEM((9, 3, 3, 8, 256), F32),
    full=VMEM((3, 2, 16, 3, 3, 8, 256), F32),
    pages=VMEM((2, 768, 256), BF),
    psem=pltpu.SemaphoreType.DMA((2,)),
    z=pltpu.SemaphoreType.DMA((2, 9)),
    y1=pltpu.SemaphoreType.DMA((2, 27)),
    y2=pltpu.SemaphoreType.DMA((2, 27)),
    y3=pltpu.SemaphoreType.DMA((2, 27)),
    gp=VMEM((3, 2, 64, 128), F32),
    gr0=VMEM((3, 64, 128), F32),
    ga=VMEM((4, 3, 64, 128), F32),
    y4=pltpu.SemaphoreType.DMA((2, 27)),
    gr=VMEM((3, 3, 3, 64, 128), F32),
    gfull=VMEM((2, 3, 64, 128), F32),
    total=VMEM((256, 256), F32),
    root=VMEM((256, 256), F32),
    matrix=VMEM((256, 256), F32),
    igv=VMEM((2048, 256), BF),
    sems=pltpu.SemaphoreType.DMA((N_SENDS,)),
    rsems=pltpu.SemaphoreType.DMA((N_SENDS,)),
    lsem=pltpu.SemaphoreType.DMA((16,)),
)


class Refs:
    pass


def step_kernel(g, own, act, damping, ig, out, *scratch):
    r = Refs()
    for name, ref in zip(SCRATCH, scratch):
        setattr(r, name, ref)
    at = place()
    f, h, w = lax.axis_index("frame"), lax.axis_index("height"), lax.axis_index("width")
    hu, hd, wl, wr = (h + 7) % 8, (h + 1) % 8, (w + 7) % 8, (w + 1) % 8
    up, down, left, right = (f, hu, w), (f, hd, w), (f, h, wl), (f, h, wr)
    across = (1 - f, h, w)
    corners = [(f, hd, wr), (f, hd, wl), (f, hu, wr), (f, hu, wl)]
    core = at["c"]
    partner = other_core(at)
    parts = (r.k0, r.k1, r.k2)
    mine = [[at[axis] for axis in o] for o in ORDERS]
    sent, kept = [], []

    def plan(src, dst, to):
        n = len(sent)
        sent.append(
            pltpu.make_async_remote_copy(
                src_ref=src,
                dst_ref=dst,
                send_sem=r.sems.at[n],
                recv_sem=r.rsems.at[n],
                device_id=to,
                device_id_type=MESH,
            )
        )
        return sent[-1]

    def go(src, dst, to):
        copy = plan(src, dst, to)
        copy.start()
        return copy

    def keep(src, dst):
        copy = pltpu.make_async_copy(src, dst, r.lsem.at[len(kept)])
        copy.start()
        kept.append(copy)
        return copy

    def three(src, dst, p, s):
        return [go(src(k), dst(k), along(at, ORDERS[p][s], k)) for k in (1, 2, 3)]

    def landed(copies):
        for copy in copies:
            copy.wait_recv()

    index = [m[2] * 16 + m[1] * 4 + m[0] for m in mine]
    inside = keep(g, r.gc.at[0:4, 1:17])
    flat = keep(act, r.act)
    held_rows = keep(own, r.ownv)
    meet(
        [up, down, left, right, across, partner]
        + corners
        + [along(at, axis, k) for axis in "xyz" for k in (1, 2, 3)]
    )
    last = 3 * (1 - f)
    near = [
        go(g.at[:, 0:1], r.gc.at[0:4, 17:18], up),
        go(g.at[:, 15:16], r.gc.at[0:4, 0:1], down),
    ]
    face = [go(g.at[last], r.gc.at[4, 1:17], across)]
    line = lax.broadcasted_iota(jnp.int32, (32, 512), 0)
    spot = lax.broadcasted_iota(jnp.int32, (32, 512), 1)
    want = jnp.where(line < 16, line * 32 + 31, (line - 16) * 32)
    pick = jnp.where(spot == want, 1.0, 0.0).astype(BF)
    r.spots[...] = jnp.zeros((4, 16, 256), F32)
    held_rows.wait()
    r.o0[...] = r.ownv[0:16, :]
    r.o1[...] = r.ownv[16:32, :]
    r.mix[0:24, :] = jnp.zeros((24, 256), F32)
    r.mix[0:22, :] = r.ownv[32:54, :].astype(F32)
    r.o2[...] = r.mix[0:24, :].astype(BF)
    gather = []
    for p, rows in enumerate((r.o0, r.o1, r.o2)):
        keep(rows, parts[p].at[core, index[p]])
        gather.append(three(lambda k: rows, lambda k: parts[p].at[core, index[p]], p, 0))
    inside.wait()
    for frame in range(4):
        block = r.gc[frame, 1:17].reshape(512, 256)
        cut = jnp.dot(pick, block, preferred_element_type=F32)
        r.edge[0, frame] = cut[:16].astype(BF)
        r.edge[1, frame] = cut[16:].astype(BF)
        for kind, n in enumerate((15, 31, 0, 16)):
            r.spots[kind, frame : frame + 1, :] = cut[n : n + 1]
    r.cs[...] = r.spots[...].astype(BF)
    near += [
        go(r.edge.at[0], r.lc.at[0:4], right),
        go(r.edge.at[1], r.rc.at[0:4], left),
    ] + [go(r.cs.at[kind], r.cr.at[kind], to) for kind, to in enumerate(corners)]
    flat.wait()

    def flip(n, carry):
        rows = pl.ds(pl.multiple_of(256 * n, 256), 256)
        r.act_t[:, rows] = r.act[rows, :].astype(F32).T.astype(BF)
        return carry

    lax.fori_loop(0, 8, flip, 0)
    for copy in kept[3:6]:
        copy.wait()
    for p in range(3):
        landed(gather[p])
        held = parts[p].at[core, pl.ds(mine[p][2] * 16 + mine[p][1] * 4, 4)]
        gather[p] = three(lambda k: held, lambda k: held, p, 1)
    landed(near)
    face += [
        go(r.gc.at[last, 0:1], r.gc.at[4, 0:1], across),
        go(r.gc.at[last, 17:18], r.gc.at[4, 17:18], across),
        go(r.lc.at[last], r.lc.at[4], across),
        go(r.rc.at[last], r.rc.at[4], across),
        go(r.cr, r.cf, across),
    ]

    sub = lax.broadcasted_iota(jnp.int32, (32, 256), 0)

    def build(n, carry):
        frame, row = n // 18, n % 18
        slot = jnp.where(frame == 4, 5 * (1 - f), frame + 1)
        off = jnp.logical_or(
            jnp.logical_and(row == 0, h == 0), jnp.logical_and(row == 17, h == 7)
        )
        keep = jnp.where(off, 0.0, 1.0)
        x = r.gc[frame, row].astype(F32) * keep
        before = r.lf[frame, pl.ds(row, 1), :] * keep
        after = r.rf[frame, pl.ds(row, 1), :] * keep
        r.gs[1, slot, row] = x.astype(BF)
        r.gs[0, slot, row] = jnp.where(sub == 31, after, pltpu.roll(x, 31, 0)).astype(BF)
        r.gs[2, slot, row] = jnp.where(sub == 0, before, pltpu.roll(x, 1, 0)).astype(BF)
        return carry

    def clear(n, carry):
        for c in range(3):
            r.gs[c, 5 * f, n] = jnp.zeros((32, 256), BF)
        return carry

    def border(frame, corner):
        for side, columns, wide, edge in ((0, r.lc, r.lf, 0), (1, r.rc, r.rf, 7)):
            out = w == edge
            wide[frame, 1:17, :] = jnp.where(out, 0.0, columns[frame].astype(F32))
            wide[frame, 0:1, :] = jnp.where(out, 0.0, corner(side))
            wide[frame, 17:18, :] = jnp.where(out, 0.0, corner(2 + side))

    for frame in range(4):
        border(frame, lambda kind: r.cr[kind].astype(F32)[frame : frame + 1])
    lax.fori_loop(0, 72, build, 0)
    lax.fori_loop(0, 18, clear, 0)

    def turn_of(n):
        return jnp.where(n < 3, 3 + n, jnp.where((n < 6) == (f == 0), 6 + n % 3, n % 3))

    def nth(n):
        return jnp.where(n < 3, n + 3, jnp.where(n < 6, n - 3, n))

    def remote(src, dst, sems, n, to):
        return pltpu.make_async_remote_copy(
            src_ref=src,
            dst_ref=dst,
            send_sem=sems.at[0, n],
            recv_sem=sems.at[1, n],
            device_id=to,
            device_id_type=MESH,
        )

    def swaps(n):
        return [remote(r.kg.at[n, :, pl.ds(1 - core, 1)], r.r0.at[n], r.z, n, partner)]

    def firsts(n):
        b = n % 3
        return [
            remote(
                r.s1.at[n, :, pl.ds((turn(at, b, 0) + k) % 4, 1)],
                r.ra.at[n, k - 1],
                r.y1,
                3 * n + k - 1,
                turned(at, b, 0, k),
            )
            for k in (1, 2, 3)
        ]

    def seconds(n):
        b = n % 3
        return [
            remote(
                r.s2.at[n, :, pl.ds((turn(at, b, 1) + k) % 4, 1)],
                r.rb.at[n, k - 1],
                r.y2,
                3 * n + k - 1,
                turned(at, b, 1, k),
            )
            for k in (1, 2, 3)
        ]

    def thirds(n):
        return [
            remote(r.s3.at[n], r.r3.at[n, k - 1], r.y3, 3 * n + k - 1, turned(at, n % 3, 2, k))
            for k in (1, 2, 3)
        ]

    def start(copies):
        for copy in copies:
            copy.start()

    def weight(n):
        a, b = n // 3, n % 3
        s = jnp.concatenate(
            [r.gs[c, pl.ds(2 - a, 4), pl.ds(2 - b, 16)].reshape(2048, 256) for c in range(3)], 1
        )
        taps = jnp.dot(r.act_t[...], s, preferred_element_type=F32)
        for c in range(3):
            r.kg[n, c] = taps[:, 256 * c : 256 * c + 256].reshape(2, 4, 4, 8, 256)
        start(swaps(n))

    def first(n):
        landed(swaps(n))
        for c in range(3):
            r.s1[n, c] = r.kg[n, c, core] + r.r0[n, c, 0]
        start(firsts(n))

    def second(i, carry):
        n = nth(i)
        landed(firsts(n))
        mine_a = turn(at, n % 3, 0)
        for c in range(3):
            r.s2[n, c] = (r.s1[n, c, mine_a] + r.ra[n, 1, c, 0]) + (
                r.ra[n, 0, c, 0] + r.ra[n, 2, c, 0]
            )
        start(seconds(n))
        return carry

    def third(i, carry):
        n = nth(i)
        landed(seconds(n))
        mine_b = turn(at, n % 3, 1)
        for c in range(3):
            r.s3[n, c] = (r.s2[n, c, mine_b] + r.rb[n, 1, c, 0]) + (
                r.rb[n, 0, c, 0] + r.rb[n, 2, c, 0]
            )
        start(thirds(n))
        return carry

    def fourth(i, carry):
        n = nth(i)
        landed(thirds(n))
        a, b = n // 3, n % 3
        r.full[b, core, turn(at, b, 0) * 4 + turn(at, b, 1), a] = (r.s3[n] + r.r3[n, 1]) + (
            r.r3[n, 0] + r.r3[n, 2]
        )
        return carry

    widest = []
    for p in range(3):
        held = parts[p].at[core, pl.ds(mine[p][2] * 16, 16)]
        widest.append([plan(held, held, along(at, ORDERS[p][2], k)) for k in (1, 2, 3)])

    for p in range(3):
        landed(gather[p])
        start(widest[p])

    def chunk(n, carry):
        @pl.when(n == 6)
        def _():
            landed(face)
            far = [
                jnp.where(f == 0, r.cf[kind].astype(F32)[0:1], r.cf[kind].astype(F32)[3:4])
                for kind in range(4)
            ]
            border(4, lambda kind: far[kind])
            lax.fori_loop(72, 90, build, 0)

        @pl.when(n < 9)
        def _():
            weight(turn_of(n))

        @pl.when(n >= 1)
        def _():
            first(turn_of(n - 1))

        return carry

    lax.fori_loop(0, 10, chunk, 0)
    lax.fori_loop(0, 6, second, 0)
    lax.fori_loop(0, 3, third, 0)
    lax.fori_loop(6, 9, second, 0)
    lax.fori_loop(3, 6, third, 0)
    for p in range(3):
        landed(widest[p])
        gather[p] = [go(parts[p].at[core], parts[p].at[core], partner)]
    lax.fori_loop(0, 3, fourth, 0)
    lax.fori_loop(6, 9, third, 0)
    lax.fori_loop(3, 9, fourth, 0)

    def align(n, carry):
        x_hi, z, c = n // 8, (n // 2) % 4, n % 2
        for col in range(8):
            spot = {"x": 2 * x_hi + col % 2, "y": col // 2, "z": z}
            for p, (part, (lo, hi)) in enumerate(zip(parts, CUTS)):
                o = ORDERS[p]
                block = part[c, spot[o[2]] * 16 + spot[o[1]] * 4 + spot[o[0]]].astype(F32)
                r.mix[54 * col + lo : 54 * col + hi] = block[: hi - lo]
        r.kal[pl.ds(pl.multiple_of(n * 432, 432), 432), :] = r.mix[...].astype(BF)
        return carry

    def data(q, carry):
        taps = [
            r.gs[t % 3, q + 2 - t // 9, pl.ds(2 - (t // 3) % 3, 16)].reshape(512, 256)
            for t in range(27)
        ]
        sums = jnp.dot(jnp.concatenate(taps, 1), r.kal[...], preferred_element_type=F32)
        r.igv[pl.ds(pl.multiple_of(q * 512, 512), 512), :] = (
            sums / jnp.sqrt(jnp.float32(6912))
        ).astype(BF)
        return carry

    x = jnp.concatenate(
        [r.full[p, core, mine[p][0] * 4 + mine[p][1]].reshape(72, 256) for p in range(3)], 0
    )
    high, low = halves(x)
    grams = jnp.dot(
        x.T.astype(BF), jnp.concatenate([high, low], 1), preferred_element_type=F32
    )
    gram = 0.25 * (grams[:, :256] + (grams[:, 256:] + grams[:, 256:].T))
    for p, block in enumerate((gram[:128, :128], gram[:128, 128:], gram[128:, 128:])):
        r.gp[p] = block.reshape(2, 64, 128)
    halfgram = go(r.gp.at[:, 1 - core], r.gr0, partner)
    spread = []
    for p in range(3):
        held = r.full.at[p, core, mine[p][0] * 4 + mine[p][1]]
        spread.append(three(lambda k: held, lambda k: held, p, 1))
    for p in range(3):
        landed(gather[p])
    lax.fori_loop(0, 16, align, 0)
    landed([halfgram])
    r.ga[0] = r.gp[:, core] + r.gr0[...]

    def sums(n, carry):
        hops = [
            [
                remote(r.ga.at[n, p], r.gr.at[n, p, k - 1], r.y4, 9 * n + 3 * p + k - 1, turned(at, p, n, k))
                for k in (1, 2, 3)
            ]
            for p in range(3)
        ]
        for p in range(3):
            start(hops[p])
        data(n, 0)
        for p in range(3):
            landed(hops[p])
            r.ga[n + 1, p] = (r.ga[n, p] + r.gr[n, p, 1]) + (r.gr[n, p, 0] + r.gr[n, p, 2])
        for p in range(3):
            for copy in hops[p]:
                copy.wait_send()
        return carry

    lax.fori_loop(0, 3, sums, 0)
    r.gfull[core] = r.ga[3]
    other = go(r.gfull.at[core], r.gfull.at[core], partner)
    for p in range(3):
        landed(spread[p])
        held = r.full.at[p, core, pl.ds(mine[p][0] * 4, 4)]
        spread[p] = [
            go(held, held, along(at, ORDERS[p][0], 1)),
            go(held, held, along(at, ORDERS[p][0], 3)),
        ]
    data(3, 0)
    keep_ig = keep(r.igv, ig)
    landed([other])
    b0, b1, b2 = [r.gfull[:, p].reshape(128, 128) for p in range(3)]
    r.total[...] = jnp.concatenate(
        [jnp.concatenate([b0, b1], 1), jnp.concatenate([b1.T, b2], 1)], 0
    )

    row = lax.broadcasted_iota(jnp.int32, (256, 256), 0)
    column = lax.broadcasted_iota(jnp.int32, (256, 256), 1)
    identity = jnp.where(row == column, 1.0, 0.0).astype(F32)
    factor = r.total[...] + (damping[0, 0] / 256.0) * whole(r.total[...] * identity) * identity
    scale = 2.5 / jnp.sqrt(whole(factor * factor))
    r.root[...] = jnp.sqrt(jnp.sqrt(scale)) * identity
    r.matrix[...] = scale * factor

    relayed, doubled = [], []
    for p in range(3):
        before = r.full.at[p, core, pl.ds((mine[p][0] + 3) % 4 * 4, 2)]
        after = r.full.at[p, core, pl.ds((mine[p][0] + 1) % 4 * 4 + 2, 2)]
        relayed.append(
            [
                plan(before, before, along(at, ORDERS[p][0], 1)),
                plan(after, after, along(at, ORDERS[p][0], 3)),
            ]
        )
        doubled.append(plan(r.full.at[p, core], r.full.at[p, core], partner))

    def newton(n, carry):
        middle = (5.0 * identity - r.matrix[...]) / 4.0
        r.root[...] = product(r.root[...], middle)
        square = product(middle, middle)
        r.matrix[...] = product(square, product(square, r.matrix[...]))

        @pl.when(n == ON)
        def _():
            for p in range(3):
                landed(spread[p])
                start(relayed[p])

        @pl.when(n == OVER)
        def _():
            for p in range(3):
                landed(relayed[p])
                doubled[p].start()

        return carry

    lax.fori_loop(0, ITERS, newton, 0)
    root = r.root[...]
    energy = whole(root * product(r.total[...], root))
    size = jnp.sqrt(energy / (6912.0 * 256.0) + 1e-6)
    rh, rl = halves(root * (0.5 / size))
    stack = jnp.concatenate([rh, rl, rh], 0)

    def page(n):
        return pltpu.make_async_copy(
            r.pages.at[n % 2],
            out.at[pl.ds(pl.multiple_of(n * 768, 768), 768)],
            r.psem.at[n % 2],
        )

    def write(n, carry):
        @pl.when(n >= 2)
        def _():
            page(n - 2).wait()

        high, low = halves(
            jnp.concatenate(
                [r.full[n % 3, :, :, n // 3, c].reshape(256, 256) for c in range(3)], 0
            )
        )
        direction = jnp.dot(
            jnp.concatenate([high, high, low], 1), stack, preferred_element_type=F32
        )
        old = r.kal[pl.ds(pl.multiple_of(n * 768, 768), 768), :].astype(F32)
        r.pages[n % 2] = (old - direction).astype(BF)
        page(n).start()
        return carry

    landed(doubled)
    lax.fori_loop(0, 9, write, 0)
    page(7).wait()
    page(8).wait()
    keep_ig.wait()
    for copy in sent:
        copy.wait_send()

    def drain(n, carry):
        for copy in swaps(n) + firsts(n) + seconds(n) + thirds(n):
            copy.wait_send()
        return carry

    lax.fori_loop(0, 9, drain, 0)
    assert len(sent) <= N_SENDS, len(sent)


def step(g, own, act, damping):
    return pl.pallas_call(
        step_kernel,
        out_shape=(VMEM((2048, 256), BF), VMEM((6912, 256), BF)),
        in_specs=[pl.BlockSpec(memory_space=pl.ANY)] * 3
        + [pl.BlockSpec(memory_space=pltpu.SMEM)],
        out_specs=[pl.BlockSpec(memory_space=pl.ANY)] * 2,
        scratch_shapes=list(SCRATCH.values()),
        compiler_params=pltpu.CompilerParams(
            collective_id=0, has_side_effects=True, vmem_limit_bytes=LIMIT
        ),
        name="step",
    )(g, own, act, damping)


def on_device(activations, out_grad, kernel, damping):
    ig, new = step(
        out_grad, kernel, activations.reshape(2048, 256), damping.reshape(1, 1)
    )
    return ig.reshape(activations.shape), new


def solution(mesh):
    placed = (
        P("frame", "height", "width", None),
        P("frame", "height", "width", None),
        P(("frame", "height", "width"), None),
        P(),
    )
    return jax.shard_map(
        on_device,
        mesh=mesh,
        in_specs=placed,
        out_specs=(P("frame", "height", "width", None), P()),
        check_vma=False,
    )
```

time: 119 us -> 106 us (0.89)
  Pallas kernels: 110 us -> 102 us
  local copies, waits for them, and re-layouts: 7.65 us -> 2.77 us
    pallas_call x1, Pallas kernels: 110 us -> 102 us  [step(): pl.pallas_call(step_kernel, out_shape=(VMEM((2048, 256), BF), VMEM((6912,...]
    unnamed x2, local copies, waits for them, and re-layouts: 6.28 us -> 2.77 us
    reshape x1 -> x0, local copies, waits for them, and re-layouts: 1.36 us -> none  [on_device(): own = jnp.pad(kernel, ((0, 2), (0, 0))).reshape(7, 8, 256)]
where the time goes in v3:
time: 106 us
  Pallas kernels  102 us (96%)
  local copies, waits for them, and re-layouts  2.77 us (3%)
  between operations  1.29 us (1%)
    pallas_call x1, Pallas kernels, step(): pl.pallas_call(step_kernel, out_shape=(VMEM((2048, 256), BF), VMEM((6912,...  102 us
    unnamed x2, local copies, waits for them, and re-layouts  2.77 us

profile of v3, /device:TPU:1, one launch (start us, length us, event | category | flops | bytes accessed | tf_op | source)
XLA Modules:
  0.0 105.6 jit_solution(11803468245595943040)
XLA Ops:
  1.3 101.6 %step.1 = (bf16[2048,256]{1,0:T(8,128)(2,1)S(1)}, bf16[6912,256]{1,0:T(8,128)(2,1)S(1)}) custom-call(bf16[4,16,32,256]{3,2,1,0:T(8,128)(2,1)} %g.1, bf16[54,256]{1,0:T(8,128)(2,1)} %own.1, bf16[2048,256]{1,0:T(8,128)(2,1)} %bitcast.5, f32[1,1]{1,0:T(1,128)} %bitcast.3.damping), custom_call_target="tpu_custom_call" | custom-call | tf_op jit(solution)/shard_map/step/pallas_call | solution.py:601
  102.9 1.0 copy.8
  103.9 1.8 %copy.9 = bf16[6912,256]{1,0:T(8,128)(2,1)} copy(bf16[6912,256]{1,0:T(8,128)(2,1)S(1)} %get-tuple-element.7) | data formatting | bytes 7077888

commit v4 on v3

--- a/solution.py
+++ b/solution.py
@@ -9,7 +9,7 @@
 
 MESH = pl.DeviceIdType.MESH
 ITERS = 12
-ON, OVER = 4, 8
+AG, ON = 2, 5
 VMEM = pltpu.VMEM
 BF = jnp.bfloat16
 F32 = jnp.float32
@@ -35,11 +35,15 @@
 
 def turn(at, b, s):
     which = (b + s) % 3
+    if isinstance(which, int):
+        return at["xyz"[which]]
     return jnp.where(which == 0, at["x"], jnp.where(which == 1, at["y"], at["z"]))
 
 
 def turned(at, b, s, k):
     which, moved = (b + s) % 3, dict(at)
+    if isinstance(which, int):
+        return along(at, "xyz"[which], k)
     for n, axis in enumerate("xyz"):
         moved[axis] = jnp.where(which == n, (at[axis] + k) % 4, at[axis])
     return device(moved)
@@ -110,8 +114,9 @@
     s3=VMEM((9, 3, 8, 256), F32),
     r3=VMEM((9, 3, 3, 8, 256), F32),
     full=VMEM((3, 2, 16, 3, 3, 8, 256), F32),
-    pages=VMEM((2, 768, 256), BF),
-    psem=pltpu.SemaphoreType.DMA((2,)),
+    pages=VMEM((9, 3, 128, 256), BF),
+    psem=pltpu.SemaphoreType.DMA((9,)),
+    y5=pltpu.SemaphoreType.DMA((2, 9)),
     z=pltpu.SemaphoreType.DMA((2, 9)),
     y1=pltpu.SemaphoreType.DMA((2, 27)),
     y2=pltpu.SemaphoreType.DMA((2, 27)),
@@ -281,14 +286,23 @@
 
     for frame in range(4):
         border(frame, lambda kind: r.cr[kind].astype(F32)[frame : frame + 1])
-    lax.fori_loop(0, 72, build, 0)
+    def six(n, carry):
+        for row in range(6):
+            build(6 * n + row, carry)
+        return carry
+
+    lax.fori_loop(0, 12, six, 0)
     lax.fori_loop(0, 18, clear, 0)
 
     def turn_of(n):
         return jnp.where(n < 3, 3 + n, jnp.where((n < 6) == (f == 0), 6 + n % 3, n % 3))
 
     def nth(n):
-        return jnp.where(n < 3, n + 3, jnp.where(n < 6, n - 3, n))
+        return n + 3 if n < 3 else n - 3 if n < 6 else n
+
+    def each(low, high, step):
+        for n in range(low, high):
+            step(n)
 
     def remote(src, dst, sems, n, to):
         return pltpu.make_async_remote_copy(
@@ -355,7 +369,7 @@
             r.s1[n, c] = r.kg[n, c, core] + r.r0[n, c, 0]
         start(firsts(n))
 
-    def second(i, carry):
+    def second(i):
         n = nth(i)
         landed(firsts(n))
         mine_a = turn(at, n % 3, 0)
@@ -364,9 +378,8 @@
                 r.ra[n, 0, c, 0] + r.ra[n, 2, c, 0]
             )
         start(seconds(n))
-        return carry
-
-    def third(i, carry):
+
+    def third(i):
         n = nth(i)
         landed(seconds(n))
         mine_b = turn(at, n % 3, 1)
@@ -375,16 +388,14 @@
                 r.rb[n, 0, c, 0] + r.rb[n, 2, c, 0]
             )
         start(thirds(n))
-        return carry
-
-    def fourth(i, carry):
+
+    def fourth(i):
         n = nth(i)
         landed(thirds(n))
         a, b = n // 3, n % 3
         r.full[b, core, turn(at, b, 0) * 4 + turn(at, b, 1), a] = (r.s3[n] + r.r3[n, 1]) + (
             r.r3[n, 0] + r.r3[n, 2]
         )
-        return carry
 
     widest = []
     for p in range(3):
@@ -404,7 +415,7 @@
                 for kind in range(4)
             ]
             border(4, lambda kind: far[kind])
-            lax.fori_loop(72, 90, build, 0)
+            lax.fori_loop(12, 15, six, 0)
 
         @pl.when(n < 9)
         def _():
@@ -417,17 +428,6 @@
         return carry
 
     lax.fori_loop(0, 10, chunk, 0)
-    lax.fori_loop(0, 6, second, 0)
-    lax.fori_loop(0, 3, third, 0)
-    lax.fori_loop(6, 9, second, 0)
-    lax.fori_loop(3, 6, third, 0)
-    for p in range(3):
-        landed(widest[p])
-        gather[p] = [go(parts[p].at[core], parts[p].at[core], partner)]
-    lax.fori_loop(0, 3, fourth, 0)
-    lax.fori_loop(6, 9, third, 0)
-    lax.fori_loop(3, 9, fourth, 0)
-
     def align(n, carry):
         x_hi, z, c = n // 8, (n // 2) % 4, n % 2
         for col in range(8):
@@ -450,6 +450,23 @@
         ).astype(BF)
         return carry
 
+    for p in range(3):
+        landed(widest[p])
+        gather[p] = [go(parts[p].at[core], parts[p].at[core], partner)]
+    each(0, 6, second)
+    each(0, 3, third)
+    each(6, 9, second)
+    each(3, 6, third)
+    each(0, 3, fourth)
+    each(6, 9, third)
+    for p in range(3):
+        landed(gather[p])
+    lax.fori_loop(0, 16, align, 0)
+    for n in range(9):
+        for copy in swaps(n) + firsts(n):
+            copy.wait_send()
+    each(3, 9, fourth)
+
     x = jnp.concatenate(
         [r.full[p, core, mine[p][0] * 4 + mine[p][1]].reshape(72, 256) for p in range(3)], 0
     )
@@ -465,9 +482,21 @@
     for p in range(3):
         held = r.full.at[p, core, mine[p][0] * 4 + mine[p][1]]
         spread.append(three(lambda k: held, lambda k: held, p, 1))
-    for p in range(3):
-        landed(gather[p])
-    lax.fori_loop(0, 16, align, 0)
+    sides, relayed = [], []
+    for p in range(3):
+        axis, home = ORDERS[p][0], mine[p][0] * 4
+        before, after = (home + 12) % 16, (home + 4) % 16
+
+        def block(low, count):
+            return r.full.at[p, core, pl.ds(low, count)]
+
+        sides.append([plan(block(home, 4), block(home, 4), along(at, axis, k)) for k in (1, 3)])
+        relayed.append(
+            [
+                plan(block(before, 2), block(before, 2), along(at, axis, 1)),
+                plan(block(after + 2, 2), block(after + 2, 2), along(at, axis, 3)),
+            ]
+        )
     landed([halfgram])
     r.ga[0] = r.gp[:, core] + r.gr0[...]
 
@@ -481,6 +510,13 @@
         ]
         for p in range(3):
             start(hops[p])
+
+        @pl.when(n == AG)
+        def _():
+            for p in range(3):
+                landed(spread[p])
+                start(sides[p])
+
         data(n, 0)
         for p in range(3):
             landed(hops[p])
@@ -493,15 +529,11 @@
     lax.fori_loop(0, 3, sums, 0)
     r.gfull[core] = r.ga[3]
     other = go(r.gfull.at[core], r.gfull.at[core], partner)
-    for p in range(3):
-        landed(spread[p])
-        held = r.full.at[p, core, pl.ds(mine[p][0] * 4, 4)]
-        spread[p] = [
-            go(held, held, along(at, ORDERS[p][0], 1)),
-            go(held, held, along(at, ORDERS[p][0], 3)),
-        ]
     data(3, 0)
     keep_ig = keep(r.igv, ig)
+    for n in range(9):
+        for copy in seconds(n) + thirds(n):
+            copy.wait_send()
     landed([other])
     b0, b1, b2 = [r.gfull[:, p].reshape(128, 128) for p in range(3)]
     r.total[...] = jnp.concatenate(
@@ -516,18 +548,6 @@
     r.root[...] = jnp.sqrt(jnp.sqrt(scale)) * identity
     r.matrix[...] = scale * factor
 
-    relayed, doubled = [], []
-    for p in range(3):
-        before = r.full.at[p, core, pl.ds((mine[p][0] + 3) % 4 * 4, 2)]
-        after = r.full.at[p, core, pl.ds((mine[p][0] + 1) % 4 * 4 + 2, 2)]
-        relayed.append(
-            [
-                plan(before, before, along(at, ORDERS[p][0], 1)),
-                plan(after, after, along(at, ORDERS[p][0], 3)),
-            ]
-        )
-        doubled.append(plan(r.full.at[p, core], r.full.at[p, core], partner))
-
     def newton(n, carry):
         middle = (5.0 * identity - r.matrix[...]) / 4.0
         r.root[...] = product(r.root[...], middle)
@@ -537,14 +557,8 @@
         @pl.when(n == ON)
         def _():
             for p in range(3):
-                landed(spread[p])
+                landed(sides[p])
                 start(relayed[p])
-
-        @pl.when(n == OVER)
-        def _():
-            for p in range(3):
-                landed(relayed[p])
-                doubled[p].start()
 
         return carry
 
@@ -557,50 +571,45 @@
 
     def page(n):
         return pltpu.make_async_copy(
-            r.pages.at[n % 2],
-            out.at[pl.ds(pl.multiple_of(n * 768, 768), 768)],
-            r.psem.at[n % 2],
-        )
+            r.pages.at[n], out.at[pl.ds(3 * n, 3), core], r.psem.at[n]
+        )
+
+    def paired(n):
+        return remote(r.pages.at[n], out.at[pl.ds(3 * n, 3), core], r.y5, n, partner)
 
     def write(n, carry):
-        @pl.when(n >= 2)
-        def _():
-            page(n - 2).wait()
-
         high, low = halves(
             jnp.concatenate(
-                [r.full[n % 3, :, :, n // 3, c].reshape(256, 256) for c in range(3)], 0
+                [r.full[n % 3, core, :, n // 3, c].reshape(128, 256) for c in range(3)], 0
             )
         )
         direction = jnp.dot(
             jnp.concatenate([high, high, low], 1), stack, preferred_element_type=F32
         )
-        old = r.kal[pl.ds(pl.multiple_of(n * 768, 768), 768), :].astype(F32)
-        r.pages[n % 2] = (old - direction).astype(BF)
+        for c in range(3):
+            rows = pl.ds(pl.multiple_of(768 * n + 256 * c + 128 * core, 128), 128)
+            old = r.kal[rows, :].astype(F32)
+            r.pages[n, c] = (old - direction[128 * c : 128 * c + 128]).astype(BF)
+        paired(n).start()
         page(n).start()
         return carry
 
-    landed(doubled)
+    for p in range(3):
+        landed(relayed[p])
     lax.fori_loop(0, 9, write, 0)
-    page(7).wait()
-    page(8).wait()
+    for n in range(9):
+        page(n).wait()
+        paired(n).wait()
     keep_ig.wait()
     for copy in sent:
         copy.wait_send()
-
-    def drain(n, carry):
-        for copy in swaps(n) + firsts(n) + seconds(n) + thirds(n):
-            copy.wait_send()
-        return carry
-
-    lax.fori_loop(0, 9, drain, 0)
     assert len(sent) <= N_SENDS, len(sent)
 
 
 def step(g, own, act, damping):
     return pl.pallas_call(
         step_kernel,
-        out_shape=(VMEM((2048, 256), BF), VMEM((6912, 256), BF)),
+        out_shape=(VMEM((2048, 256), BF), VMEM((27, 2, 128, 256), BF)),
         in_specs=[pl.BlockSpec(memory_space=pl.ANY)] * 3
         + [pl.BlockSpec(memory_space=pltpu.SMEM)],
         out_specs=[pl.BlockSpec(memory_space=pl.ANY)] * 2,
@@ -616,7 +625,7 @@
     ig, new = step(
         out_grad, kernel, activations.reshape(2048, 256), damping.reshape(1, 1)
     )
-    return ig.reshape(activations.shape), new
+    return ig.reshape(activations.shape), new.reshape(6912, 256)
 
 
 def solution(mesh):

time: 106 us -> 102 us (0.962)
  Pallas kernels: 102 us -> 97.7 us
    pallas_call x1, Pallas kernels: 102 us -> 97.7 us  [step(): pl.pallas_call(step_kernel, out_shape=(VMEM((2048, 256), BF), VMEM((27, 2...]
where the time goes in v4:
time: 102 us
  Pallas kernels  97.7 us (96%)
  local copies, waits for them, and re-layouts  2.77 us (3%)
  between operations  1.29 us (1%)
    pallas_call x1, Pallas kernels, step(): pl.pallas_call(step_kernel, out_shape=(VMEM((2048, 256), BF), VMEM((27, 2...  97.7 us
    unnamed x2, local copies, waits for them, and re-layouts  2.77 us

profile of v4, /device:TPU:1, one launch (start us, length us, event | category | flops | bytes accessed | tf_op | source)
XLA Modules:
  0.0 101.8 jit_solution(10956832783418696749)
XLA Ops:
  1.3 97.7 %step.1 = (bf16[2048,256]{1,0:T(8,128)(2,1)S(1)}, bf16[27,2,128,256]{3,2,1,0:T(8,128)(2,1)S(1)}) custom-call(bf16[4,16,32,256]{3,2,1,0:T(8,128)(2,1)} %g.1, bf16[54,256]{1,0:T(8,128)(2,1)} %own.1, bf16[2048,256]{1,0:T(8,128)(2,1)} %bitcast.7, f32[1,1]{1,0:T(1,128)} %bitcast.4.damping), custom_call_target="tpu_custom_call" | custom-call | tf_op jit(solution)/shard_map/step/pallas_call | solution.py:610
  99.0 1.0 copy.8
  100.0 1.8 %copy.9 = bf16[6912,256]{1,0:T(8,128)(2,1)} copy(bf16[6912,256]{1,0:T(8,128)(2,1)S(1)} %bitcast.5) | data formatting | bytes 7077888

commit v5 on v4

--- a/solution.py
+++ b/solution.py
@@ -9,7 +9,7 @@
 
 MESH = pl.DeviceIdType.MESH
 ITERS = 12
-AG, ON = 2, 5
+PASS, AG, ON = 8, 2, 5
 VMEM = pltpu.VMEM
 BF = jnp.bfloat16
 F32 = jnp.float32
@@ -397,16 +397,33 @@
             r.r3[n, 0] + r.r3[n, 2]
         )
 
-    widest = []
-    for p in range(3):
-        held = parts[p].at[core, pl.ds(mine[p][2] * 16, 16)]
-        widest.append([plan(held, held, along(at, ORDERS[p][2], k)) for k in (1, 2, 3)])
+    widest, onward = [], []
+    for p in range(3):
+        axis, home = ORDERS[p][2], mine[p][2] * 16
+        before, after = (home + 48) % 64, (home + 16) % 64
+
+        def slots(low, count):
+            return parts[p].at[core, pl.ds(low, count)]
+
+        widest.append([plan(slots(home, 16), slots(home, 16), along(at, axis, k)) for k in (1, 3)])
+        onward.append(
+            [
+                plan(slots(before, 8), slots(before, 8), along(at, axis, 1)),
+                plan(slots(after + 8, 8), slots(after + 8, 8), along(at, axis, 3)),
+            ]
+        )
 
     for p in range(3):
         landed(gather[p])
         start(widest[p])
 
     def chunk(n, carry):
+        @pl.when(n == PASS)
+        def _():
+            for p in range(3):
+                landed(widest[p])
+                start(onward[p])
+
         @pl.when(n == 6)
         def _():
             landed(face)
@@ -451,7 +468,7 @@
         return carry
 
     for p in range(3):
-        landed(widest[p])
+        landed(onward[p])
         gather[p] = [go(parts[p].at[core], parts[p].at[core], partner)]
     each(0, 6, second)
     each(0, 3, third)

time: 102 us -> 100 us (0.980)
  Pallas kernels: 97.7 us -> 96.2 us
    pallas_call x1, Pallas kernels: 97.7 us -> 96.2 us  [step(): pl.pallas_call(step_kernel, out_shape=(VMEM((2048, 256), BF), VMEM((27, 2...]
where the time goes in v5:
time: 100 us
  Pallas kernels  96.2 us (96%)
  local copies, waits for them, and re-layouts  2.77 us (3%)
  between operations  1.29 us (1%)
    pallas_call x1, Pallas kernels, step(): pl.pallas_call(step_kernel, out_shape=(VMEM((2048, 256), BF), VMEM((27, 2...  96.2 us
    unnamed x2, local copies, waits for them, and re-layouts  2.77 us

profile of v5, /device:TPU:1, one launch (start us, length us, event | category | flops | bytes accessed | tf_op | source)
XLA Modules:
  0.0 100.3 jit_solution(13033102352959931587)
XLA Ops:
  1.3 96.2 %step.1 = (bf16[2048,256]{1,0:T(8,128)(2,1)S(1)}, bf16[27,2,128,256]{3,2,1,0:T(8,128)(2,1)S(1)}) custom-call(bf16[4,16,32,256]{3,2,1,0:T(8,128)(2,1)} %g.1, bf16[54,256]{1,0:T(8,128)(2,1)} %own.1, bf16[2048,256]{1,0:T(8,128)(2,1)} %bitcast.7, f32[1,1]{1,0:T(1,128)} %bitcast.4.damping), custom_call_target="tpu_custom_call" | custom-call | tf_op jit(solution)/shard_map/step/pallas_call | solution.py:627
  97.5 1.0 copy.8
  98.5 1.8 %copy.9 = bf16[6912,256]{1,0:T(8,128)(2,1)} copy(bf16[6912,256]{1,0:T(8,128)(2,1)S(1)} %bitcast.5) | data formatting | bytes 7077888
